TPU v7x, 32 devices: a whole 2x2x4 slice. The times are simulated.
32 devices in a mesh: group: 2 (over x), expert: 16 (over z, y, core).
Axes of the slice: x: 2, y: 2, z: 4, core: 2. Of those that a mesh axis runs over, the one named last changes fastest.
Arguments:
- tokens: bfloat16 [128, 7168], P(('group', 'expert')), parts along dimension 0, may hold values from -6 to 6
- expert_ids: int32 [128, 2], P(('group', 'expert')), parts along dimension 0, may hold values from 0 to 1, all different within a row; in each aligned block of 4 rows (0 to 3, 4 to 7, ...) at most 4 rows name the same one
- gate_codes: int32 [128, 2], P(('group', 'expert')), parts along dimension 0, may hold values from 1 to 65535
- gate_weight: bfloat16 [16, 7168, 256], P('expert'), may hold values from -0.0625 to 0.0625
- up_weight: bfloat16 [16, 7168, 256], P('expert'), may hold values from -0.0625 to 0.0625
- down_weight: bfloat16 [16, 256, 7168], P('expert'), may hold values from -0.125 to 0.125
- target_basis: bfloat16 [7168, 512], P('expert'), may hold values from -0.0625 to 0.0625
Outputs:
- targets: bfloat16 [128, 512], P(('group', 'expert')), parts along dimension 0
There are 2 independent parts, one for each index of `group`. A program takes and returns all parts, laid end to end along the dimension named above; an argument that names none is the same for every part. Nothing has to cross between parts.
Inputs may be any that keep to these rules, and one draw needn't show every extreme that they name: `expert_ids`: each row names 2 different experts; among the 4 rows of one device no expert is named more than 4 times, a bound that some block reaches.
All inputs are finite; a program needn't handle non-finite values.
Results may differ from a plain program's by a relative error of at most 0.0057.
Values may be sent and summed in bfloat16 or wider, within the bound.
No kernel may reach another device: no remote copies, remote signals or barrier semaphores. Data moves between devices by JAX's collectives and lax.ppermute only.
A program may use at most 128 MiB of HBM per device.

v0:
```python
import functools

import jax
import jax.numpy as jnp
from jax import lax
from jax.experimental import pallas as pl
from jax.experimental.pallas import tpu as pltpu
from jax.sharding import PartitionSpec as P


SLICES = 8
CORES = 2
COLUMNS = 2
MAX_PLANES = 4
FETCH_PARTS = 8
LANES = 128
MIB = 1 << 20


def run_expert(received, gate_weight, up_weight, down_weight):
    sources, slots, feature_width = received.shape
    row_block = received.reshape(sources * slots, feature_width)
    gate_act = jnp.dot(row_block, gate_weight[0], preferred_element_type=jnp.float32)
    up_act = jnp.dot(row_block, up_weight[0], preferred_element_type=jnp.float32)
    hidden = (jax.nn.silu(gate_act) * up_act).astype(jnp.bfloat16)
    expert_part = jnp.dot(hidden, down_weight[0], preferred_element_type=jnp.float32).astype(
        jnp.bfloat16
    )
    return expert_part.reshape(sources, slots, feature_width)


def general_shards(
    tokens, expert_ids, gate_codes, gate_weight, up_weight, down_weight, target_basis
):
    token_count, feature_width = tokens.shape
    pick_count = expert_ids.shape[1]
    owner_count = lax.axis_size("expert")
    expert_count = owner_count // SLICES
    capacity = min(token_count, max(2, 5 * token_count * pick_count // (4 * expert_count)))
    rank_width = target_basis.shape[1]
    flat_ids = expert_ids.reshape(-1)
    onehot = (flat_ids[:, None] == jnp.arange(expert_count, dtype=jnp.int32)[None, :]).astype(
        jnp.int32
    )
    before = jnp.cumsum(onehot, axis=0) - onehot
    slot_rank = jnp.sum(before * onehot, axis=1)
    slot_index = flat_ids * capacity + slot_rank
    row_token = jnp.arange(token_count * pick_count, dtype=jnp.int32) // pick_count
    slot_table = (
        jnp.full((expert_count * capacity,), token_count, jnp.int32).at[slot_index].set(row_token)
    )
    padded = jnp.concatenate([tokens, jnp.zeros((1, feature_width), tokens.dtype)], axis=0)
    per_expert_rows = padded[slot_table].reshape(expert_count, 1, capacity, feature_width)
    outgoing = jnp.broadcast_to(per_expert_rows, (expert_count, SLICES, capacity, feature_width))
    outgoing = outgoing.reshape(owner_count, capacity, feature_width)
    full_basis = lax.all_gather(target_basis, "expert", axis=0, tiled=True)
    expert_part = run_expert(
        lax.all_to_all(outgoing, "expert", split_axis=0, concat_axis=0, tiled=True),
        gate_weight,
        up_weight,
        down_weight,
    )
    result = jnp.einsum("skd,dr->skr", expert_part, full_basis, preferred_element_type=jnp.float32)
    returned = lax.all_to_all(result, "expert", split_axis=0, concat_axis=0, tiled=True)
    summed = jnp.sum(returned.reshape(expert_count, SLICES, capacity, rank_width), axis=1)
    projected = summed.reshape(expert_count * capacity, rank_width)[slot_index]
    codes_float = gate_codes.astype(jnp.float32)
    weights = 2.5 * codes_float / jnp.sum(codes_float, axis=1, keepdims=True)
    projected = projected.reshape(token_count, pick_count, rank_width)
    return jnp.sum(weights[:, :, None] * projected, axis=1).astype(jnp.bfloat16)


def fetch_kernel(index_ref, *refs):
    del index_ref
    sems = refs[-1]
    count, parts = sems.shape
    copies = []
    for k in range(parts):
        for w in range(count):
            source, target = refs[w], refs[count + w]
            rows = target.shape[0] // parts
            part = pl.ds(k * rows, rows)
            copies.append(
                pltpu.make_async_copy(source.at[0, part, :], target.at[part, :], sems.at[w, k])
            )
            copies[-1].start()
    for copy in copies:
        copy.wait()


def stack_tokens_kernel(rows_at, *refs):
    for at, block in zip(rows_at, refs[:-1]):
        rows = block.shape[0]
        refs[-1][at : at + rows, :] = block[...]


def plane_of(index):
    return jnp.right_shift(index, (CORES * COLUMNS).bit_length() - 1)


def place_of(index):
    return jnp.bitwise_and(index, CORES * COLUMNS - 1)


def expert_kernel(order, index_ref, *refs):
    places = CORES * COLUMNS
    stacks = refs[:places]
    gate_ref, up_ref, down_ref = refs[places : places + 3]
    pieces = refs[places + 3 : -1]
    x_ref = refs[-1]
    planes = len(order)
    quarter, width = stacks[0].shape
    rows = quarter // planes
    total = places * quarter
    span = width // planes
    me = plane_of(index_ref[0])
    for b, stack in enumerate(stacks):
        x_ref[b * quarter : (b + 1) * quarter, :] = stack[...]
    x = x_ref[...]
    gate_act = jnp.dot(x, gate_ref[...], preferred_element_type=jnp.float32)
    up_act = jnp.dot(x, up_ref[...], preferred_element_type=jnp.float32)
    hidden = (gate_act / (1.0 + jnp.exp(-gate_act)) * up_act).astype(jnp.bfloat16)
    to_row = lax.broadcasted_iota(jnp.int32, (total, total), 0)
    from_row = lax.broadcasted_iota(jnp.int32, (total, total), 1)
    wanted = jnp.bitwise_xor(from_row, me * rows)
    plane_order = jnp.where(to_row == wanted, 1.0, 0.0).astype(jnp.bfloat16)
    hidden = jnp.dot(plane_order, hidden, preferred_element_type=jnp.float32).astype(jnp.bfloat16)
    for n, step in enumerate(order):
        at = pl.multiple_of(jnp.bitwise_xor(me, step) * span, LANES)
        out = jnp.dot(hidden, down_ref[:, pl.ds(at, span)], preferred_element_type=jnp.float32)
        out = out.astype(jnp.bfloat16)
        for p, piece in enumerate(pieces):
            piece[n] = out[p * quarter : (p + 1) * quarter]


def stack_kernel(index_ref, *refs):
    shards_in, out_ref = refs[:-1], refs[-1]
    rows = shards_in[0].shape[0]
    for b, shard in enumerate(shards_in):
        at = pl.multiple_of(jnp.bitwise_xor(place_of(index_ref[0]), b) * rows, rows)
        out_ref[pl.ds(at, rows), :] = shard[...]


def part_total(at, own_ref, other_ref, crossed_ref):
    total = own_ref[at].astype(jnp.float32) + other_ref[at].astype(jnp.float32)
    first = own_ref.shape[0] - crossed_ref.shape[0]
    return total + crossed_ref[max(at - first, 0)].astype(jnp.float32)


def total_kernel(at, own_ref, other_ref, crossed_ref, out_ref):
    out_ref[...] = part_total(at, own_ref, other_ref, crossed_ref).astype(out_ref.dtype)


def basis_kernel(per, index_ref, own_ref, other_ref, crossed_ref, *refs):
    planes = (len(refs) - 2) // 2
    parts, basis_ref = refs[: planes - 1], refs[planes - 1]
    outs, s_ref, o_ref = refs[planes:-2], refs[-2], refs[-1]
    quarter = crossed_ref.shape[1]
    experts = planes // per
    rows = quarter // planes
    me = plane_of(index_ref[0])
    for e in range(experts):
        total = part_total(planes - 1, own_ref, other_ref, crossed_ref) if e == 0 else 0.0
        for d in range(max(1, e * per), (e + 1) * per):
            total += parts[d - 1][...].astype(jnp.float32)
        high = total.astype(jnp.bfloat16)
        low = (total - high.astype(jnp.float32)).astype(jnp.bfloat16)
        at = pl.multiple_of(jnp.bitwise_xor(me // per, e) * quarter, quarter)
        s_ref[pl.ds(at, quarter), :] = high
        s_ref[pl.ds(experts * quarter + at, quarter), :] = low
    out = jnp.dot(s_ref[...], basis_ref[...], preferred_element_type=jnp.float32)
    out = out[: experts * quarter] + out[experts * quarter :]
    for e in range(experts):
        for p in range(planes):
            at = e * quarter + p * rows
            o_ref[p, e * rows : (e + 1) * rows, :] = out[at : at + rows]
    for d in range(planes):
        outs[d][...] = o_ref[jnp.bitwise_xor(me, d)]


def sharded_basis_shards(
    tokens, expert_ids, gate_codes, gate_weight, up_weight, down_weight, target_basis
):
    rows, width = tokens.shape
    devices = lax.axis_size("expert")
    place_count = CORES * COLUMNS
    planes = devices // place_count
    experts = devices // SLICES
    quarter = planes * rows
    span = width // planes
    rank = target_basis.shape[1]
    index = lax.axis_index("expert").astype(jnp.int32).reshape(1)
    bf16 = jnp.bfloat16

    def swap(x, step):
        return lax.ppermute(x, "expert", [(i, i ^ step) for i in range(devices)])

    def core_swap(x):
        return swap(x, 1)

    def column_swap(x):
        return swap(x, CORES)

    def plane_swap(x, step):
        return swap(x, place_count * step) if step else x

    vmem = pl.BlockSpec(memory_space=pltpu.VMEM)
    smem = pl.BlockSpec(memory_space=pltpu.SMEM)

    order = sorted(range(planes), key=lambda d: (d < planes // 2, d))
    order = order[: planes // 2] + order[: planes // 2 - 1 : -1]
    near = {d: plane_swap(tokens, d) for d in order}
    far = {d: column_swap(near[d]) for d in order}
    stacks = []
    for blocks in (near, far):
        stacks.append(
            pl.pallas_call(
                functools.partial(stack_tokens_kernel, [d * rows for d in order]),
                out_shape=jax.ShapeDtypeStruct((quarter, width), bf16),
                in_specs=[vmem] * planes,
                out_specs=vmem,
                compiler_params=pltpu.CompilerParams(vmem_limit_bytes=4 * MIB),
                name="stack_tokens",
            )(*[blocks[d] for d in order])
        )
    stacks += [core_swap(stack) for stack in stacks]

    basis_shards = [target_basis, core_swap(target_basis)]
    column_basis = column_swap(target_basis)
    basis_shards += [column_basis, core_swap(column_basis)]

    fetched = []
    for group in ((gate_weight, up_weight), (down_weight,)):
        group = [pltpu.with_memory_space_constraint(w, pltpu.HBM) for w in group]
        fetched += pl.pallas_call(
            fetch_kernel,
            out_shape=tuple(pltpu.VMEM(w.shape[1:], w.dtype) for w in group),
            in_specs=[smem] + [pl.BlockSpec(memory_space=pltpu.HBM)] * len(group),
            out_specs=(vmem,) * len(group),
            scratch_shapes=[pltpu.SemaphoreType.DMA((len(group), FETCH_PARTS))],
            compiler_params=pltpu.CompilerParams(vmem_limit_bytes=MIB),
        )(index, *group)
    fetched = [pltpu.with_memory_space_constraint(w, pltpu.VMEM) for w in fetched]
    piece = jax.ShapeDtypeStruct((planes, quarter, span), bf16)
    pieces = pl.pallas_call(
        functools.partial(expert_kernel, order),
        out_shape=(piece,) * place_count,
        in_specs=[smem] + [vmem] * (place_count + 3),
        out_specs=(vmem,) * place_count,
        scratch_shapes=[pltpu.VMEM((place_count * quarter, width), bf16)],
        compiler_params=pltpu.CompilerParams(vmem_limit_bytes=16 * MIB),
        name="expert_work",
    )(index, *stacks, *fetched)

    basis = pl.pallas_call(
        stack_kernel,
        out_shape=jax.ShapeDtypeStruct((width // planes, rank), bf16),
        in_specs=[smem] + [vmem] * place_count,
        out_specs=vmem,
        compiler_params=pltpu.CompilerParams(vmem_limit_bytes=8 * MIB),
        name="stack_basis",
    )(index, *basis_shards)

    own_own, own_far, other_own, other_far = pieces
    other_far = core_swap(other_far)
    other_own = core_swap(other_own)
    pairs = (own_far.astype(jnp.float32) + other_far.astype(jnp.float32)).astype(bf16)
    crossed = {}
    for n, d in enumerate(order):
        if d >= planes // 2:
            crossed[d] = column_swap(pairs[n : n + 1])
    rest = column_swap(pairs[len(crossed) :])
    crossed.update({d: rest for d in range(planes // 2)})
    parts = []
    for d in range(1, planes):
        total = pl.pallas_call(
            functools.partial(total_kernel, order.index(d)),
            out_shape=jax.ShapeDtypeStruct((quarter, span), bf16),
            in_specs=[vmem] * 3,
            out_specs=vmem,
            compiler_params=pltpu.CompilerParams(vmem_limit_bytes=4 * MIB),
        )(own_own, other_own, crossed[d])
        parts.append(plane_swap(total, d))
    out_piece = jax.ShapeDtypeStruct((experts * rows, rank), jnp.float32)
    partial = pl.pallas_call(
        functools.partial(basis_kernel, SLICES // place_count),
        out_shape=(out_piece,) * planes,
        in_specs=[smem] + [vmem] * (planes + 3),
        out_specs=(vmem,) * planes,
        scratch_shapes=[
            pltpu.VMEM((2 * experts * quarter, span), bf16),
            pltpu.VMEM((planes, experts * rows, rank), jnp.float32),
        ],
        compiler_params=pltpu.CompilerParams(vmem_limit_bytes=16 * MIB),
        name="basis_product",
    )(index, own_own, other_own, crossed[0], *parts, basis)
    projected = sum(plane_swap(partial[d], d) for d in order)
    projected = projected.reshape(experts, rows, rank)
    codes_float = gate_codes.astype(jnp.float32)
    gates = 2.5 * codes_float / jnp.sum(codes_float, axis=1, keepdims=True)
    chosen = expert_ids[None, :, :] == jnp.arange(experts, dtype=jnp.int32)[:, None, None]
    per_expert = jnp.sum(jnp.where(chosen, gates[None, :, :], 0.0), axis=2)
    return jnp.sum(per_expert[:, :, None] * projected, axis=0).astype(bf16)


def fits(tokens, target_basis):
    rows, width = tokens.shape
    devices = lax.axis_size("expert")
    planes = devices // (CORES * COLUMNS)
    return (
        devices % SLICES == 0
        and SLICES % (CORES * COLUMNS) == 0
        and planes & (planes - 1) == 0
        and 1 < planes <= MAX_PLANES
        and rows & (rows - 1) == 0
        and planes * rows % 16 == 0
        and width % (planes * LANES) == 0
        and target_basis.shape[0] * devices == width
        and target_basis.shape[0] % 16 == 0
    )


def shards(tokens, expert_ids, gate_codes, gate_weight, up_weight, down_weight, target_basis):
    plan = sharded_basis_shards if fits(tokens, target_basis) else general_shards
    return plan(tokens, expert_ids, gate_codes, gate_weight, up_weight, down_weight, target_basis)


def solution(mesh):
    in_specs = (
        P(("group", "expert"), None),
        P(("group", "expert"), None),
        P(("group", "expert"), None),
        P("expert", None, None),
        P("expert", None, None),
        P("expert", None, None),
        P("expert", None),
    )
    out_specs = P(("group", "expert"), None)
    return jax.shard_map(shards, mesh=mesh, in_specs=in_specs, out_specs=out_specs, check_vma=False)
```

profile of v0, /device:TPU:0, one launch (start us, length us, event | category | flops | bytes accessed | tf_op | source)
XLA Modules:
  0.0 53.9 jit_solution(3918728627309310275)
XLA Ops:
  0.0 4.1 %collective-permute-start = (bf16[4,7168]{1,0:T(4,128)(2,1)}, bf16[4,7168]{1,0:T(4,128)(2,1)S(1)}, u32[]{:S(2)}, u32[]{:S(2)}) collective-permute-start(bf16[4,7168]{1,0:T(4,128)(2,1)} %refs_3_.1), channel_id=1, source_target_pairs={{0,8},{1,9},{2,10},{3,11},{4,12},{5,13},{6,14},{7,15},{8,0},{9,1},... | collective-permute-start | bytes 172040 | tf_op jit(solution)/shard_map/ppermute | solution.py:196
  4.1 1.3 %collective-permute-start.1 = (bf16[4,7168]{1,0:T(4,128)(2,1)}, bf16[4,7168]{1,0:T(4,128)(2,1)S(1)}, u32[]{:S(2)}, u32[]{:S(2)}) collective-permute-start(bf16[4,7168]{1,0:T(4,128)(2,1)} %refs_3_.1), channel_id=1, source_target_pairs={{0,12},{1,13},{2,14},{3,15},{4,8},{5,9},{6,10},{7,11},{8,4},{9,5},... | collective-permute-start | bytes 172040 | tf_op jit(solution)/shard_map/ppermute | solution.py:196
  5.6 1.5 %collective-permute-start.6 = (bf16[4,7168]{1,0:T(4,128)(2,1)}, bf16[4,7168]{1,0:T(4,128)(2,1)S(1)}, u32[]{:S(2)}, u32[]{:S(2)}) collective-permute-start(bf16[4,7168]{1,0:T(4,128)(2,1)} %refs_3_.1), channel_id=1, source_target_pairs={{0,2},{1,3},{2,0},{3,1},{4,6},{5,7},{6,4},{7,5},{8,10},{9,11},{10,... | collective-permute-start | bytes 172040 | tf_op jit(solution)/shard_map/ppermute | solution.py:196
  7.2 1.6 %collective-permute-start.3 = (bf16[4,7168]{1,0:T(4,128)(2,1)S(1)}, bf16[4,7168]{1,0:T(4,128)(2,1)S(1)}, u32[]{:S(2)}, u32[]{:S(2)}) collective-permute-start(bf16[4,7168]{1,0:T(4,128)(2,1)S(1)} %collective-permute-done.refs_0_), channel_id=1, source_target_pairs={{0,2},{1,3},{2,0},{3,1},{4,6},{5,7},{6,4},{7,5},{8,10},{9,11},{10,... | collective-permute-start | bytes 172040 | tf_op jit(solution)/shard_map/ppermute | solution.py:196
  8.8 1.6 %collective-permute-done.1.refs_1_ = bf16[4,7168]{1,0:T(4,128)(2,1)S(1)} collective-permute-done((bf16[4,7168]{1,0:T(4,128)(2,1)}, bf16[4,7168]{1,0:T(4,128)(2,1)S(1)}, u32[]{:S(2)}, u32[]{:S(2)}) %collective-permute-start.1) | collective-permute-done | bytes 57376 | tf_op jit(solution)/shard_map/ppermute | solution.py:196
  10.4 1.5 %collective-permute-start.4 = (bf16[4,7168]{1,0:T(4,128)(2,1)S(1)}, bf16[4,7168]{1,0:T(4,128)(2,1)S(1)}, u32[]{:S(2)}, u32[]{:S(2)}) collective-permute-start(bf16[4,7168]{1,0:T(4,128)(2,1)S(1)} %collective-permute-done.1.refs_1_), channel_id=1, source_target_pairs={{0,2},{1,3},{2,0},{3,1},{4,6},{5,7},{6,4},{7,5},{8,10},{9,11},{10,... | collective-permute-start | bytes 172040 | tf_op jit(solution)/shard_map/ppermute | solution.py:196
  12.4 0.8 %copy-done.1 = bf16[4,7168]{1,0:T(4,128)(2,1)S(1)} copy-done((bf16[4,7168]{1,0:T(4,128)(2,1)S(1)}, bf16[4,7168]{1,0:T(4,128)(2,1)}, u32[]{:S(2)}) %copy-start.1) | copy-done | bytes 57368
  13.4 1.2 %collective-permute-done.4.refs_1_ = bf16[4,7168]{1,0:T(4,128)(2,1)S(1)} collective-permute-done((bf16[4,7168]{1,0:T(4,128)(2,1)S(1)}, bf16[4,7168]{1,0:T(4,128)(2,1)S(1)}, u32[]{:S(2)}, u32[]{:S(2)}) %collective-permute-start.4) | collective-permute-done | bytes 57376 | tf_op jit(solution)/shard_map/ppermute | solution.py:196
  14.5 1.5 %collective-permute-done.5.refs_2_ = bf16[4,7168]{1,0:T(4,128)(2,1)S(1)} collective-permute-done((bf16[4,7168]{1,0:T(4,128)(2,1)S(1)}, bf16[4,7168]{1,0:T(4,128)(2,1)S(1)}, u32[]{:S(2)}, u32[]{:S(2)}) %collective-permute-start.5) | collective-permute-done | bytes 57376 | tf_op jit(solution)/shard_map/ppermute | solution.py:196
  16.9 2.1 %shard_map.74.refs_6_ = bf16[256,7168]{1,0:T(8,128)(2,1)S(1)} custom-call(s32[1]{0:T(128)} %bitcast.index_ref, bf16[1,256,7168]{2,1,0:T(8,128)(2,1)} %refs_0_.4), custom_call_target="tpu_custom_call" | custom-call | tf_op jit(solution)/shard_map/pallas_call | solution.py:235
  18.9 3.2 %shard_map.73 = (bf16[7168,256]{1,0:T(8,128)(2,1)S(1)}, bf16[7168,256]{1,0:T(8,128)(2,1)S(1)}) custom-call(s32[1]{0:T(128)} %bitcast.index_ref, bf16[1,7168,256]{2,1,0:T(8,128)(2,1)} %refs_0_.3, bf16[1,7168,256]{2,1,0:T(8,128)(2,1)} %refs_1_.1), custom_call_target="tpu_custom_call" | custom-call | tf_op jit(solution)/shard_map/pallas_call | solution.py:235
  22.2 2.3 %expert_work.1 = (bf16[4,16,1792]{2,1,0:T(8,128)(2,1)S(1)}, bf16[4,16,1792]{2,1,0:T(8,128)(2,1)S(1)}, bf16[4,16,1792]{2,1,0:T(8,128)(2,1)S(1)}, bf16[4,16,1792]{2,1,0:T(8,128)(2,1)S(1)}) custom-call(s32[1]{0:T(128)} %bitcast.index_ref, bf16[16,7168]{1,0:T(8,128)(2,1)S(1)} %stack_tokens.2.refs_0_, bf16[16,7168]{1,0:T(8,128)(2,1)S(1)} %stack_tokens.3.refs_1_, ...), custom_call_target="tpu_custom_call" | custom-call | tf_op jit(solution)/shard_map/expert_work/pallas_call | solution.py:245
  25.2 4.1 %collective-permute-done.18.refs_2_ = bf16[448,512]{1,0:T(8,128)(2,1)S(1)} collective-permute-done((bf16[448,512]{1,0:T(8,128)(2,1)}, bf16[448,512]{1,0:T(8,128)(2,1)S(1)}, u32[]{:S(2)}, u32[]{:S(2)}) %collective-permute-start.18) | collective-permute-done | bytes 458784 | tf_op jit(solution)/shard_map/ppermute | solution.py:196
  30.1 1.5 %collective-permute-start.15 = (bf16[1,16,1792]{2,1,0:T(8,128)(2,1)S(1)}, bf16[1,16,1792]{2,1,0:T(8,128)(2,1)S(1)}, u32[]{:S(2)}, u32[]{:S(2)}) collective-permute-start(bf16[1,16,1792]{2,1,0:T(8,128)(2,1)S(1)} %get-tuple-element.25), channel_id=1, source_target_pairs={{0,2},{1,3},{2,0},{3,1},{4,6},{5,7},{6,4},{7,5},{8,10},{9,11},{10,... | collective-permute-start | bytes 172040 | tf_op jit(solution)/shard_map/ppermute | solution.py:196
  32.2 4.5 %collective-permute-done.15.crossed_ref = bf16[1,16,1792]{2,1,0:T(8,128)(2,1)S(1)} collective-permute-done((bf16[1,16,1792]{2,1,0:T(8,128)(2,1)S(1)}, bf16[1,16,1792]{2,1,0:T(8,128)(2,1)S(1)}, u32[]{:S(2)}, u32[]{:S(2)}) %collective-permute-start.15) | collective-permute-done | bytes 57376 | tf_op jit(solution)/shard_map/ppermute | solution.py:196
  36.8 3.0 %collective-permute-start.16 = (bf16[16,1792]{1,0:T(8,128)(2,1)S(1)}, bf16[16,1792]{1,0:T(8,128)(2,1)S(1)}, u32[]{:S(2)}, u32[]{:S(2)}) collective-permute-start(bf16[16,1792]{1,0:T(8,128)(2,1)S(1)} %shard_map.77), channel_id=1, source_target_pairs={{0,12},{1,13},{2,14},{3,15},{4,8},{5,9},{6,10},{7,11},{8,4},{9,5},... | collective-permute-start | bytes 172040 | tf_op jit(solution)/shard_map/ppermute | solution.py:196
  39.9 1.5 %collective-permute-start.12 = (bf16[16,1792]{1,0:T(8,128)(2,1)S(1)}, bf16[16,1792]{1,0:T(8,128)(2,1)S(1)}, u32[]{:S(2)}, u32[]{:S(2)}) collective-permute-start(bf16[16,1792]{1,0:T(8,128)(2,1)S(1)} %shard_map.75), channel_id=1, source_target_pairs={{0,4},{1,5},{2,6},{3,7},{4,0},{5,1},{6,2},{7,3},{8,12},{9,13},{10,... | collective-permute-start | bytes 172040 | tf_op jit(solution)/shard_map/ppermute | solution.py:196
  41.6 1.4 %collective-permute-done.16.refs_2_ = bf16[16,1792]{1,0:T(8,128)(2,1)S(1)} collective-permute-done((bf16[16,1792]{1,0:T(8,128)(2,1)S(1)}, bf16[16,1792]{1,0:T(8,128)(2,1)S(1)}, u32[]{:S(2)}, u32[]{:S(2)}) %collective-permute-start.16) | collective-permute-done | bytes 57376 | tf_op jit(solution)/shard_map/ppermute | solution.py:196
  42.9 2.2 %collective-permute-done.14.refs_1_ = bf16[16,1792]{1,0:T(8,128)(2,1)S(1)} collective-permute-done((bf16[16,1792]{1,0:T(8,128)(2,1)S(1)}, bf16[16,1792]{1,0:T(8,128)(2,1)S(1)}, u32[]{:S(2)}, u32[]{:S(2)}) %collective-permute-start.14) | collective-permute-done | bytes 57376 | tf_op jit(solution)/shard_map/ppermute | solution.py:196
  45.7 1.9 %collective-permute-start.20 = (f32[8,512]{1,0:T(8,128)S(1)}, f32[8,512]{1,0:T(8,128)S(1)}, u32[]{:S(2)}, u32[]{:S(2)}) collective-permute-start(f32[8,512]{1,0:T(8,128)S(1)} %get-tuple-element.21), channel_id=1, source_target_pairs={{0,8},{1,9},{2,10},{3,11},{4,12},{5,13},{6,14},{7,15},{8,0},{9,1},... | collective-permute-start | bytes 49160 | tf_op jit(solution)/shard_map/ppermute | solution.py:196
  47.6 0.9 %collective-permute-start.21 = (f32[8,512]{1,0:T(8,128)S(1)}, f32[8,512]{1,0:T(8,128)S(1)}, u32[]{:S(2)}, u32[]{:S(2)}) collective-permute-start(f32[8,512]{1,0:T(8,128)S(1)} %get-tuple-element.22), channel_id=1, source_target_pairs={{0,12},{1,13},{2,14},{3,15},{4,8},{5,9},{6,10},{7,11},{8,4},{9,5},... | collective-permute-start | bytes 49160 | tf_op jit(solution)/shard_map/ppermute | solution.py:196
  48.5 0.7 %collective-permute-start.22 = (f32[8,512]{1,0:T(8,128)S(1)}, f32[8,512]{1,0:T(8,128)S(1)}, u32[]{:S(2)}, u32[]{:S(2)}) collective-permute-start(f32[8,512]{1,0:T(8,128)S(1)} %get-tuple-element.23), channel_id=1, source_target_pairs={{0,4},{1,5},{2,6},{3,7},{4,0},{5,1},{6,2},{7,3},{8,12},{9,13},{10,... | collective-permute-start | bytes 49160 | tf_op jit(solution)/shard_map/ppermute | solution.py:196
  49.3 1.5 %collective-permute-done.20 = f32[8,512]{1,0:T(8,128)S(1)} collective-permute-done((f32[8,512]{1,0:T(8,128)S(1)}, f32[8,512]{1,0:T(8,128)S(1)}, u32[]{:S(2)}, u32[]{:S(2)}) %collective-permute-start.20) | collective-permute-done | bytes 16416 | tf_op jit(solution)/shard_map/ppermute | solution.py:196
  50.7 2.4 %collective-permute-done.21 = f32[8,512]{1,0:T(8,128)S(1)} collective-permute-done((f32[8,512]{1,0:T(8,128)S(1)}, f32[8,512]{1,0:T(8,128)S(1)}, u32[]{:S(2)}, u32[]{:S(2)}) %collective-permute-start.21) | collective-permute-done | bytes 16416 | tf_op jit(solution)/shard_map/ppermute | solution.py:196
  (49 shorter events, 5.3 us)
Async XLA Ops:
  0.0 7.2 %collective-permute-start = (bf16[4,7168]{1,0:T(4,128)(2,1)}, bf16[4,7168]{1,0:T(4,128)(2,1)S(1)}, u32[]{:S(2)}, u32[]{:S(2)}) collective-permute-start(bf16[4,7168]{1,0:T(4,128)(2,1)} %refs_3_.1), channel_id=1, source_target_pairs={{0,8},{1,9},{2,10},{3,11},{4,12},{5,13},{6,14},{7,15},{8,0},{9,1},... | collective-permute-start | bytes 172040 | tf_op jit(solution)/shard_map/ppermute | solution.py:196
  4.1 6.3 %collective-permute-start.1 = (bf16[4,7168]{1,0:T(4,128)(2,1)}, bf16[4,7168]{1,0:T(4,128)(2,1)S(1)}, u32[]{:S(2)}, u32[]{:S(2)}) collective-permute-start(bf16[4,7168]{1,0:T(4,128)(2,1)} %refs_3_.1), channel_id=1, source_target_pairs={{0,12},{1,13},{2,14},{3,15},{4,8},{5,9},{6,10},{7,11},{8,4},{9,5},... | collective-permute-start | bytes 172040 | tf_op jit(solution)/shard_map/ppermute | solution.py:196
  5.4 6.5 %collective-permute-start.2 = (bf16[4,7168]{1,0:T(4,128)(2,1)}, bf16[4,7168]{1,0:T(4,128)(2,1)S(1)}, u32[]{:S(2)}, u32[]{:S(2)}) collective-permute-start(bf16[4,7168]{1,0:T(4,128)(2,1)} %refs_3_.1), channel_id=1, source_target_pairs={{0,4},{1,5},{2,6},{3,7},{4,0},{5,1},{6,2},{7,3},{8,12},{9,13},{10,... | collective-permute-start | bytes 172040 | tf_op jit(solution)/shard_map/ppermute | solution.py:196
  5.6 7.7 %collective-permute-start.6 = (bf16[4,7168]{1,0:T(4,128)(2,1)}, bf16[4,7168]{1,0:T(4,128)(2,1)S(1)}, u32[]{:S(2)}, u32[]{:S(2)}) collective-permute-start(bf16[4,7168]{1,0:T(4,128)(2,1)} %refs_3_.1), channel_id=1, source_target_pairs={{0,2},{1,3},{2,0},{3,1},{4,6},{5,7},{6,4},{7,5},{8,10},{9,11},{10,... | collective-permute-start | bytes 172040 | tf_op jit(solution)/shard_map/ppermute | solution.py:196
  7.2 6.2 %collective-permute-start.3 = (bf16[4,7168]{1,0:T(4,128)(2,1)S(1)}, bf16[4,7168]{1,0:T(4,128)(2,1)S(1)}, u32[]{:S(2)}, u32[]{:S(2)}) collective-permute-start(bf16[4,7168]{1,0:T(4,128)(2,1)S(1)} %collective-permute-done.refs_0_), channel_id=1, source_target_pairs={{0,2},{1,3},{2,0},{3,1},{4,6},{5,7},{6,4},{7,5},{8,10},{9,11},{10,... | collective-permute-start | bytes 172040 | tf_op jit(solution)/shard_map/ppermute | solution.py:196
  10.4 4.2 %collective-permute-start.4 = (bf16[4,7168]{1,0:T(4,128)(2,1)S(1)}, bf16[4,7168]{1,0:T(4,128)(2,1)S(1)}, u32[]{:S(2)}, u32[]{:S(2)}) collective-permute-start(bf16[4,7168]{1,0:T(4,128)(2,1)S(1)} %collective-permute-done.1.refs_1_), channel_id=1, source_target_pairs={{0,2},{1,3},{2,0},{3,1},{4,6},{5,7},{6,4},{7,5},{8,10},{9,11},{10,... | collective-permute-start | bytes 172040 | tf_op jit(solution)/shard_map/ppermute | solution.py:196
  11.9 4.2 %collective-permute-start.5 = (bf16[4,7168]{1,0:T(4,128)(2,1)S(1)}, bf16[4,7168]{1,0:T(4,128)(2,1)S(1)}, u32[]{:S(2)}, u32[]{:S(2)}) collective-permute-start(bf16[4,7168]{1,0:T(4,128)(2,1)S(1)} %collective-permute-done.2.refs_2_), channel_id=1, source_target_pairs={{0,2},{1,3},{2,0},{3,1},{4,6},{5,7},{6,4},{7,5},{8,10},{9,11},{10,... | collective-permute-start | bytes 172040 | tf_op jit(solution)/shard_map/ppermute | solution.py:196
  13.3 8.9 %collective-permute-start.7 = (bf16[16,7168]{1,0:T(8,128)(2,1)S(1)}, bf16[16,7168]{1,0:T(8,128)(2,1)S(1)}, u32[]{:S(2)}, u32[]{:S(2)}) collective-permute-start(bf16[16,7168]{1,0:T(8,128)(2,1)S(1)} %stack_tokens.2.refs_0_), channel_id=1, source_target_pairs={{0,1},{1,0},{2,3},{3,2},{4,5},{5,4},{6,7},{7,6},{8,9},{9,8},{10,11... | collective-permute-start | bytes 688136 | tf_op jit(solution)/shard_map/ppermute | solution.py:196
  16.1 6.1 %collective-permute-start.8 = (bf16[16,7168]{1,0:T(8,128)(2,1)S(1)}, bf16[16,7168]{1,0:T(8,128)(2,1)S(1)}, u32[]{:S(2)}, u32[]{:S(2)}) collective-permute-start(bf16[16,7168]{1,0:T(8,128)(2,1)S(1)} %stack_tokens.3.refs_1_), channel_id=1, source_target_pairs={{0,1},{1,0},{2,3},{3,2},{4,5},{5,4},{6,7},{7,6},{8,9},{9,8},{10,11... | collective-permute-start | bytes 688136 | tf_op jit(solution)/shard_map/ppermute | solution.py:196
  16.2 13.1 %collective-permute-start.18 = (bf16[448,512]{1,0:T(8,128)(2,1)}, bf16[448,512]{1,0:T(8,128)(2,1)S(1)}, u32[]{:S(2)}, u32[]{:S(2)}) collective-permute-start(bf16[448,512]{1,0:T(8,128)(2,1)} %refs_0_.5), channel_id=1, source_target_pairs={{0,2},{1,3},{2,0},{3,1},{4,6},{5,7},{6,4},{7,5},{8,10},{9,11},{10,... | collective-permute-start | bytes 1376264 | tf_op jit(solution)/shard_map/ppermute | solution.py:196
  24.5 4.9 %collective-permute-start.10 = (bf16[4,16,1792]{2,1,0:T(8,128)(2,1)S(1)}, bf16[4,16,1792]{2,1,0:T(8,128)(2,1)S(1)}, u32[]{:S(2)}, u32[]{:S(2)}) collective-permute-start(bf16[4,16,1792]{2,1,0:T(8,128)(2,1)S(1)} %get-tuple-element.20), channel_id=1, source_target_pairs={{0,1},{1,0},{2,3},{3,2},{4,5},{5,4},{6,7},{7,6},{8,9},{9,8},{10,11... | collective-permute-start | bytes 688136 | tf_op jit(solution)/shard_map/ppermute | solution.py:196
  24.7 16.7 %collective-permute-start.17 = (bf16[448,512]{1,0:T(8,128)(2,1)S(1)}, bf16[448,512]{1,0:T(8,128)(2,1)S(1)}, u32[]{:S(2)}, u32[]{:S(2)}) collective-permute-start(bf16[448,512]{1,0:T(8,128)(2,1)S(1)} %copy-done), channel_id=1, source_target_pairs={{0,1},{1,0},{2,3},{3,2},{4,5},{5,4},{6,7},{7,6},{8,9},{9,8},{10,11... | collective-permute-start | bytes 1376264 | tf_op jit(solution)/shard_map/ppermute | solution.py:196
  25.1 6.5 %collective-permute-start.9 = (bf16[4,16,1792]{2,1,0:T(8,128)(2,1)S(1)}, bf16[4,16,1792]{2,1,0:T(8,128)(2,1)S(1)}, u32[]{:S(2)}, u32[]{:S(2)}) collective-permute-start(bf16[4,16,1792]{2,1,0:T(8,128)(2,1)S(1)} %get-tuple-element.18), channel_id=1, source_target_pairs={{0,1},{1,0},{2,3},{3,2},{4,5},{5,4},{6,7},{7,6},{8,9},{9,8},{10,11... | collective-permute-start | bytes 688136 | tf_op jit(solution)/shard_map/ppermute | solution.py:196
  29.3 12.1 %collective-permute-start.19 = (bf16[448,512]{1,0:T(8,128)(2,1)S(1)}, bf16[448,512]{1,0:T(8,128)(2,1)S(1)}, u32[]{:S(2)}, u32[]{:S(2)}) collective-permute-start(bf16[448,512]{1,0:T(8,128)(2,1)S(1)} %collective-permute-done.18.refs_2_), channel_id=1, source_target_pairs={{0,1},{1,0},{2,3},{3,2},{4,5},{5,4},{6,7},{7,6},{8,9},{9,8},{10,11... | collective-permute-start | bytes 1376264 | tf_op jit(solution)/shard_map/ppermute | solution.py:196
  29.4 10.4 %collective-permute-start.11 = (bf16[2,16,1792]{2,1,0:T(8,128)(2,1)S(1)}, bf16[2,16,1792]{2,1,0:T(8,128)(2,1)S(1)}, u32[]{:S(2)}, u32[]{:S(2)}) collective-permute-start(bf16[2,16,1792]{2,1,0:T(8,128)(2,1)S(1)} %slice.12), channel_id=1, source_target_pairs={{0,2},{1,3},{2,0},{3,1},{4,6},{5,7},{6,4},{7,5},{8,10},{9,11},{10,... | collective-permute-start | bytes 344072 | tf_op jit(solution)/shard_map/ppermute | solution.py:196
  30.1 6.6 %collective-permute-start.15 = (bf16[1,16,1792]{2,1,0:T(8,128)(2,1)S(1)}, bf16[1,16,1792]{2,1,0:T(8,128)(2,1)S(1)}, u32[]{:S(2)}, u32[]{:S(2)}) collective-permute-start(bf16[1,16,1792]{2,1,0:T(8,128)(2,1)S(1)} %get-tuple-element.25), channel_id=1, source_target_pairs={{0,2},{1,3},{2,0},{3,1},{4,6},{5,7},{6,4},{7,5},{8,10},{9,11},{10,... | collective-permute-start | bytes 172040 | tf_op jit(solution)/shard_map/ppermute | solution.py:196
  31.6 8.1 %collective-permute-start.13 = (bf16[1,16,1792]{2,1,0:T(8,128)(2,1)S(1)}, bf16[1,16,1792]{2,1,0:T(8,128)(2,1)S(1)}, u32[]{:S(2)}, u32[]{:S(2)}) collective-permute-start(bf16[1,16,1792]{2,1,0:T(8,128)(2,1)S(1)} %get-tuple-element.26), channel_id=1, source_target_pairs={{0,2},{1,3},{2,0},{3,1},{4,6},{5,7},{6,4},{7,5},{8,10},{9,11},{10,... | collective-permute-start | bytes 172040 | tf_op jit(solution)/shard_map/ppermute | solution.py:196
  36.8 12.5 %copy-start.2 = (s32[4,2]{0,1:T(2,128)S(1)}, s32[4,2]{0,1:T(2,128)}, u32[]{:S(2)}) copy-start(s32[4,2]{0,1:T(2,128)} %param.8) | copy-start | bytes 100
  36.8 6.1 %collective-permute-start.16 = (bf16[16,1792]{1,0:T(8,128)(2,1)S(1)}, bf16[16,1792]{1,0:T(8,128)(2,1)S(1)}, u32[]{:S(2)}, u32[]{:S(2)}) collective-permute-start(bf16[16,1792]{1,0:T(8,128)(2,1)S(1)} %shard_map.77), channel_id=1, source_target_pairs={{0,12},{1,13},{2,14},{3,15},{4,8},{5,9},{6,10},{7,11},{8,4},{9,5},... | collective-permute-start | bytes 172040 | tf_op jit(solution)/shard_map/ppermute | solution.py:196
  39.8 5.4 %collective-permute-start.14 = (bf16[16,1792]{1,0:T(8,128)(2,1)S(1)}, bf16[16,1792]{1,0:T(8,128)(2,1)S(1)}, u32[]{:S(2)}, u32[]{:S(2)}) collective-permute-start(bf16[16,1792]{1,0:T(8,128)(2,1)S(1)} %shard_map.76), channel_id=1, source_target_pairs={{0,8},{1,9},{2,10},{3,11},{4,12},{5,13},{6,14},{7,15},{8,0},{9,1},... | collective-permute-start | bytes 172040 | tf_op jit(solution)/shard_map/ppermute | solution.py:196
  39.9 5.3 %collective-permute-start.12 = (bf16[16,1792]{1,0:T(8,128)(2,1)S(1)}, bf16[16,1792]{1,0:T(8,128)(2,1)S(1)}, u32[]{:S(2)}, u32[]{:S(2)}) collective-permute-start(bf16[16,1792]{1,0:T(8,128)(2,1)S(1)} %shard_map.75), channel_id=1, source_target_pairs={{0,4},{1,5},{2,6},{3,7},{4,0},{5,1},{6,2},{7,3},{8,12},{9,13},{10,... | collective-permute-start | bytes 172040 | tf_op jit(solution)/shard_map/ppermute | solution.py:196
  45.7 5.0 %collective-permute-start.20 = (f32[8,512]{1,0:T(8,128)S(1)}, f32[8,512]{1,0:T(8,128)S(1)}, u32[]{:S(2)}, u32[]{:S(2)}) collective-permute-start(f32[8,512]{1,0:T(8,128)S(1)} %get-tuple-element.21), channel_id=1, source_target_pairs={{0,8},{1,9},{2,10},{3,11},{4,12},{5,13},{6,14},{7,15},{8,0},{9,1},... | collective-permute-start | bytes 49160 | tf_op jit(solution)/shard_map/ppermute | solution.py:196
  47.6 5.5 %collective-permute-start.21 = (f32[8,512]{1,0:T(8,128)S(1)}, f32[8,512]{1,0:T(8,128)S(1)}, u32[]{:S(2)}, u32[]{:S(2)}) collective-permute-start(f32[8,512]{1,0:T(8,128)S(1)} %get-tuple-element.22), channel_id=1, source_target_pairs={{0,12},{1,13},{2,14},{3,15},{4,8},{5,9},{6,10},{7,11},{8,4},{9,5},... | collective-permute-start | bytes 49160 | tf_op jit(solution)/shard_map/ppermute | solution.py:196
  48.5 4.6 %collective-permute-start.22 = (f32[8,512]{1,0:T(8,128)S(1)}, f32[8,512]{1,0:T(8,128)S(1)}, u32[]{:S(2)}, u32[]{:S(2)}) collective-permute-start(f32[8,512]{1,0:T(8,128)S(1)} %get-tuple-element.23), channel_id=1, source_target_pairs={{0,4},{1,5},{2,6},{3,7},{4,0},{5,1},{6,2},{7,3},{8,12},{9,13},{10,... | collective-permute-start | bytes 49160 | tf_op jit(solution)/shard_map/ppermute | solution.py:196
  (3 other events, 13.3 us)
where the time goes:
time: 54 us; the launch traced here: 53.9 us
  starting transfers between devices  23.2 us (43%)
  waiting for transfers between devices  20.4 us (38%)
  Pallas kernels  8.36 us (15%)
  local copies, waits for them, and re-layouts  0.87 us (2%)
  other arithmetic  0.78 us (1%)
    ppermute x23, starting transfers between devices, swap(): return lax.ppermute(x, 'expert', [(i, i ^ step) for i in range(devices)])  23.2 us
    ppermute x23, waiting for transfers between devices, swap(): return lax.ppermute(x, 'expert', [(i, i ^ step) for i in range(devices)])  20.4 us
    pallas_call x2, Pallas kernels, sharded_basis_shards(): pl.pallas_call(fetch_kernel, out_shape=tuple((pltpu.VMEM(w.shape[1:], w.d...  5.27 us
    pallas_call x1, Pallas kernels, sharded_basis_shards(): pl.pallas_call(functools.partial(expert_kernel, order), out_shape=(piece,...  2.26 us
  transfers between devices with their start and end apart: 23, of which 9 were waited for; matrix products, arithmetic and copies ran while one was open for 0% of the time, Pallas kernels for 15%

commit v1 on v0

--- a/solution.py
+++ b/solution.py
@@ -70,28 +70,44 @@
     return jnp.sum(weights[:, :, None] * projected, axis=1).astype(jnp.bfloat16)
 
 
-def fetch_kernel(index_ref, *refs):
+def fetch_kernel(parts, index_ref, *refs):
     del index_ref
-    sems = refs[-1]
-    count, parts = sems.shape
+    sources, targets, sems = refs[: len(parts)], refs[len(parts) : -1], refs[-1]
     copies = []
-    for k in range(parts):
-        for w in range(count):
-            source, target = refs[w], refs[count + w]
-            rows = target.shape[0] // parts
-            part = pl.ds(k * rows, rows)
-            copies.append(
-                pltpu.make_async_copy(source.at[0, part, :], target.at[part, :], sems.at[w, k])
-            )
+    for source, target, count in zip(sources, targets, parts):
+        rows = target.shape[0] // count
+        for k in range(count):
+            block = pl.ds(k * rows, rows)
+            sem = sems.at[len(copies)]
+            copies.append(pltpu.make_async_copy(source.at[block, :], target.at[block, :], sem))
             copies[-1].start()
     for copy in copies:
         copy.wait()
 
 
-def stack_tokens_kernel(rows_at, *refs):
-    for at, block in zip(rows_at, refs[:-1]):
+def split_kernel(source, *refs):
+    targets, sems = refs[:-1], refs[-1]
+    copies, at = [], 0
+    for n, target in enumerate(targets):
+        rows = target.shape[0]
+        copies.append(pltpu.make_async_copy(source.at[pl.ds(at, rows), :], target, sems.at[n]))
+        copies[n].start()
+        at += rows
+    for copy in copies:
+        copy.wait()
+
+
+def stack_blocks_kernel(*refs):
+    for n, block in enumerate(refs[:-1]):
+        refs[-1][n] = block[...]
+
+
+def stack_rows_kernel(sources, *refs):
+    out_ref = refs[-1]
+    for n, (ref, at) in enumerate(sources):
+        block = refs[ref][...] if at is None else refs[ref][at]
         rows = block.shape[0]
-        refs[-1][at : at + rows, :] = block[...]
+        out_ref[n * rows : (n + 1) * rows, :] = block
 
 
 def plane_of(index):
@@ -133,18 +149,20 @@
             piece[n] = out[p * quarter : (p + 1) * quarter]
 
 
-def stack_kernel(index_ref, *refs):
-    shards_in, out_ref = refs[:-1], refs[-1]
-    rows = shards_in[0].shape[0]
-    for b, shard in enumerate(shards_in):
-        at = pl.multiple_of(jnp.bitwise_xor(place_of(index_ref[0]), b) * rows, rows)
-        out_ref[pl.ds(at, rows), :] = shard[...]
+def stack_kernel(shard, index_ref, *refs):
+    out_ref = refs[-1]
+    place = place_of(index_ref[0])
+    taken = 0
+    for part in refs[:-1]:
+        rows = part.shape[0]
+        at = jnp.bitwise_xor(place, taken // shard) * shard + taken % shard
+        out_ref[pl.ds(pl.multiple_of(at, 16), rows), :] = part[...]
+        taken += rows
 
 
 def part_total(at, own_ref, other_ref, crossed_ref):
     total = own_ref[at].astype(jnp.float32) + other_ref[at].astype(jnp.float32)
-    first = own_ref.shape[0] - crossed_ref.shape[0]
-    return total + crossed_ref[max(at - first, 0)].astype(jnp.float32)
+    return total + crossed_ref[at % crossed_ref.shape[0]].astype(jnp.float32)
 
 
 def total_kernel(at, own_ref, other_ref, crossed_ref, out_ref):
@@ -210,37 +228,71 @@
     order = sorted(range(planes), key=lambda d: (d < planes // 2, d))
     order = order[: planes // 2] + order[: planes // 2 - 1 : -1]
     near = {d: plane_swap(tokens, d) for d in order}
-    far = {d: column_swap(near[d]) for d in order}
-    stacks = []
-    for blocks in (near, far):
-        stacks.append(
-            pl.pallas_call(
-                functools.partial(stack_tokens_kernel, [d * rows for d in order]),
-                out_shape=jax.ShapeDtypeStruct((quarter, width), bf16),
-                in_specs=[vmem] * planes,
-                out_specs=vmem,
-                compiler_params=pltpu.CompilerParams(vmem_limit_bytes=4 * MIB),
-                name="stack_tokens",
-            )(*[blocks[d] for d in order])
-        )
-    stacks += [core_swap(stack) for stack in stacks]
-
-    basis_shards = [target_basis, core_swap(target_basis)]
-    column_basis = column_swap(target_basis)
-    basis_shards += [column_basis, core_swap(column_basis)]
-
-    fetched = []
-    for group in ((gate_weight, up_weight), (down_weight,)):
-        group = [pltpu.with_memory_space_constraint(w, pltpu.HBM) for w in group]
-        fetched += pl.pallas_call(
-            fetch_kernel,
-            out_shape=tuple(pltpu.VMEM(w.shape[1:], w.dtype) for w in group),
-            in_specs=[smem] + [pl.BlockSpec(memory_space=pltpu.HBM)] * len(group),
-            out_specs=(vmem,) * len(group),
-            scratch_shapes=[pltpu.SemaphoreType.DMA((len(group), FETCH_PARTS))],
+    own_far = column_swap(tokens)
+
+    hbm = pl.BlockSpec(memory_space=pltpu.HBM)
+
+    def fetch(parts, *operands):
+        operands = [pltpu.with_memory_space_constraint(x, pltpu.HBM) for x in operands]
+        out = pl.pallas_call(
+            functools.partial(fetch_kernel, parts),
+            out_shape=tuple(pltpu.VMEM(x.shape, x.dtype) for x in operands),
+            in_specs=[smem] + [hbm] * len(operands),
+            out_specs=(vmem,) * len(operands),
+            scratch_shapes=[pltpu.SemaphoreType.DMA((sum(parts),))],
             compiler_params=pltpu.CompilerParams(vmem_limit_bytes=MIB),
-        )(index, *group)
-    fetched = [pltpu.with_memory_space_constraint(w, pltpu.VMEM) for w in fetched]
+        )(index, *operands)
+        return [pltpu.with_memory_space_constraint(x, pltpu.VMEM) for x in out]
+
+    gate, up, own = fetch((FETCH_PARTS, FETCH_PARTS, 1), gate_weight[0], up_weight[0], tokens)
+    (down,) = fetch((FETCH_PARTS,), down_weight[0])
+
+    def stack(kernel, shape, blocks):
+        return pl.pallas_call(
+            kernel,
+            out_shape=jax.ShapeDtypeStruct(shape, bf16),
+            in_specs=[vmem] * len(blocks),
+            out_specs=vmem,
+            compiler_params=pltpu.CompilerParams(vmem_limit_bytes=4 * MIB),
+            name="stack_tokens",
+        )(*blocks)
+
+    relayed = stack(
+        stack_blocks_kernel, (planes - 1, rows, width), [near[d] for d in range(1, planes)]
+    )
+    relayed = column_swap(relayed)
+    stacks = [
+        stack(
+            functools.partial(stack_rows_kernel, [(d, None) for d in range(planes)]),
+            (quarter, width),
+            [own] + [near[d] for d in range(1, planes)],
+        ),
+        stack(
+            functools.partial(
+                stack_rows_kernel, [(0, None)] + [(1, d) for d in range(planes - 1)]
+            ),
+            (quarter, width),
+            [own_far, relayed],
+        ),
+    ]
+    stacks += [core_swap(tokens_stack) for tokens_stack in stacks]
+
+    shard = target_basis.shape[0]
+    late = shard // 64 * 16
+    basis_parts = pl.pallas_call(
+        split_kernel,
+        out_shape=tuple(pltpu.VMEM((n, rank), bf16) for n in (shard - late, late)),
+        in_specs=[hbm],
+        out_specs=(vmem,) * 2,
+        scratch_shapes=[pltpu.SemaphoreType.DMA((2,))],
+        compiler_params=pltpu.CompilerParams(vmem_limit_bytes=MIB),
+        name="split_basis",
+    )(pltpu.with_memory_space_constraint(target_basis, pltpu.HBM))
+    column_parts = [column_swap(x) for x in basis_parts]
+    basis_shards = [
+        *basis_parts, core_swap(target_basis), *column_parts, *[core_swap(x) for x in column_parts]
+    ]
+
     piece = jax.ShapeDtypeStruct((planes, quarter, span), bf16)
     pieces = pl.pallas_call(
         functools.partial(expert_kernel, order),
@@ -250,12 +302,12 @@
         scratch_shapes=[pltpu.VMEM((place_count * quarter, width), bf16)],
         compiler_params=pltpu.CompilerParams(vmem_limit_bytes=16 * MIB),
         name="expert_work",
-    )(index, *stacks, *fetched)
+    )(index, *stacks, gate, up, down)
 
     basis = pl.pallas_call(
-        stack_kernel,
+        functools.partial(stack_kernel, shard),
         out_shape=jax.ShapeDtypeStruct((width // planes, rank), bf16),
-        in_specs=[smem] + [vmem] * place_count,
+        in_specs=[smem] + [vmem] * len(basis_shards),
         out_specs=vmem,
         compiler_params=pltpu.CompilerParams(vmem_limit_bytes=8 * MIB),
         name="stack_basis",
@@ -265,12 +317,8 @@
     other_far = core_swap(other_far)
     other_own = core_swap(other_own)
     pairs = (own_far.astype(jnp.float32) + other_far.astype(jnp.float32)).astype(bf16)
-    crossed = {}
-    for n, d in enumerate(order):
-        if d >= planes // 2:
-            crossed[d] = column_swap(pairs[n : n + 1])
-    rest = column_swap(pairs[len(crossed) :])
-    crossed.update({d: rest for d in range(planes // 2)})
+    far_count = planes // 2
+    crossed = [column_swap(pairs[:far_count]), column_swap(pairs[far_count:])]
     parts = []
     for d in range(1, planes):
         total = pl.pallas_call(
@@ -279,7 +327,7 @@
             in_specs=[vmem] * 3,
             out_specs=vmem,
             compiler_params=pltpu.CompilerParams(vmem_limit_bytes=4 * MIB),
-        )(own_own, other_own, crossed[d])
+        )(own_own, other_own, crossed[d < far_count])
         parts.append(plane_swap(total, d))
     out_piece = jax.ShapeDtypeStruct((experts * rows, rank), jnp.float32)
     partial = pl.pallas_call(
@@ -293,7 +341,7 @@
         ],
         compiler_params=pltpu.CompilerParams(vmem_limit_bytes=16 * MIB),
         name="basis_product",
-    )(index, own_own, other_own, crossed[0], *parts, basis)
+    )(index, own_own, other_own, crossed[1], *parts, basis)
     projected = sum(plane_swap(partial[d], d) for d in order)
     projected = projected.reshape(experts, rows, rank)
     codes_float = gate_codes.astype(jnp.float32)

time: 54 us -> 53.2 us (0.985)
  Pallas kernels: 8.36 us -> 9.37 us
  starting transfers between devices: 23.2 us -> 22.2 us
  local copies, waits for them, and re-layouts: 0.87 us -> 0.05 us
    pallas_call x5 -> x7, Pallas kernels: 5.52 us -> 6.56 us  [the longest x2 5.27 us: fetch(): pl.pallas_call(functools.partial(fetch_kernel, parts), out_shape=tuple((p...]
    ppermute x23 -> x22, starting transfers between devices: 23.2 us -> 22.2 us  [swap(): return lax.ppermute(x, 'expert', [(i, i ^ step) for i in range(devices)])]
    unnamed x8 -> x6, local copies, waits for them, and re-layouts: 0.84 us -> 0.02 us
    ppermute x23 -> x22, waiting for transfers between devices: 20.4 us -> 20.5 us  [swap(): return lax.ppermute(x, 'expert', [(i, i ^ step) for i in range(devices)])]
  transfers between devices with their start and end apart: 23 -> 22, of which waited for: 9 -> 11; matrix products, arithmetic and copies ran while one was open for 0% -> 0% of each run, Pallas kernels for 15% -> 17%
where the time goes in v1:
time: 53.2 us; the launch traced here: 53 us
  starting transfers between devices  22.2 us (42%)
  waiting for transfers between devices  20.5 us (39%)
  Pallas kernels  9.37 us (18%)
  other arithmetic  0.78 us (1%)
    ppermute x22, starting transfers between devices, swap(): return lax.ppermute(x, 'expert', [(i, i ^ step) for i in range(devices)])  22.2 us
    ppermute x22, waiting for transfers between devices, swap(): return lax.ppermute(x, 'expert', [(i, i ^ step) for i in range(devices)])  20.5 us
    pallas_call x2, Pallas kernels, fetch(): pl.pallas_call(functools.partial(fetch_kernel, parts), out_shape=tuple((p...  5.27 us
    pallas_call x1, Pallas kernels, sharded_basis_shards(): pl.pallas_call(functools.partial(expert_kernel, order), out_shape=(piece,...  2.24 us
  transfers between devices with their start and end apart: 22, of which 11 were waited for; matrix products, arithmetic and copies ran while one was open for 0% of the time, Pallas kernels for 17%

profile of v1, /device:TPU:0, one launch (start us, length us, event | category | flops | bytes accessed | tf_op | source)
XLA Modules:
  0.0 53.0 jit_solution(10795855036654323821)
XLA Ops:
  0.0 3.1 %collective-permute-start = (bf16[4,7168]{1,0:T(4,128)(2,1)}, bf16[4,7168]{1,0:T(4,128)(2,1)S(1)}, u32[]{:S(2)}, u32[]{:S(2)}) collective-permute-start(bf16[4,7168]{1,0:T(4,128)(2,1)} %refs_2_.1), channel_id=1, source_target_pairs={{0,4},{1,5},{2,6},{3,7},{4,0},{5,1},{6,2},{7,3},{8,12},{9,13},{10,... | collective-permute-start | bytes 172040 | tf_op jit(solution)/shard_map/ppermute | solution.py:214
  3.1 2.6 %collective-permute-start.1 = (bf16[4,7168]{1,0:T(4,128)(2,1)}, bf16[4,7168]{1,0:T(4,128)(2,1)S(1)}, u32[]{:S(2)}, u32[]{:S(2)}) collective-permute-start(bf16[4,7168]{1,0:T(4,128)(2,1)} %refs_2_.1), channel_id=1, source_target_pairs={{0,8},{1,9},{2,10},{3,11},{4,12},{5,13},{6,14},{7,15},{8,0},{9,1},... | collective-permute-start | bytes 172040 | tf_op jit(solution)/shard_map/ppermute | solution.py:214
  5.6 3.8 %collective-permute-done.1.refs_2_.refs_1_ = bf16[4,7168]{1,0:T(4,128)(2,1)S(1)} collective-permute-done((bf16[4,7168]{1,0:T(4,128)(2,1)}, bf16[4,7168]{1,0:T(4,128)(2,1)S(1)}, u32[]{:S(2)}, u32[]{:S(2)}) %collective-permute-start.1) | collective-permute-done | bytes 57376 | tf_op jit(solution)/shard_map/ppermute | solution.py:214
  9.5 2.4 %collective-permute-done.2.refs_3_.refs_2_ = bf16[4,7168]{1,0:T(4,128)(2,1)S(1)} collective-permute-done((bf16[4,7168]{1,0:T(4,128)(2,1)}, bf16[4,7168]{1,0:T(4,128)(2,1)S(1)}, u32[]{:S(2)}, u32[]{:S(2)}) %collective-permute-start.2) | collective-permute-done | bytes 57376 | tf_op jit(solution)/shard_map/ppermute | solution.py:214
  11.8 1.6 %collective-permute-start.4 = (bf16[3,4,7168]{2,1,0:T(4,128)(2,1)S(1)}, bf16[3,4,7168]{2,1,0:T(4,128)(2,1)S(1)}, u32[]{:S(2)}, u32[]{:S(2)}) collective-permute-start(bf16[3,4,7168]{2,1,0:T(4,128)(2,1)S(1)} %stack_tokens.4), channel_id=1, source_target_pairs={{0,2},{1,3},{2,0},{3,1},{4,6},{5,7},{6,4},{7,5},{8,10},{9,11},{10,... | collective-permute-start | bytes 516104 | tf_op jit(solution)/shard_map/ppermute | solution.py:214
  13.9 3.2 %shard_map.73 = (bf16[7168,256]{1,0:T(8,128)(2,1)S(1)}, bf16[7168,256]{1,0:T(8,128)(2,1)S(1)}, bf16[4,7168]{1,0:T(4,128)(2,1)S(1)}) custom-call(s32[1]{0:T(128)} %bitcast.index_ref, bf16[7168,256]{1,0:T(8,128)(2,1)} %bitcast.4, bf16[7168,256]{1,0:T(8,128)(2,1)} %bitcast.5, bf16[4,7168]{1,0:T(4,128)(2,1)} %refs_2_.1), custom_call_target="tpu_custom_call" | custom-call | tf_op jit(solution)/shard_map/pallas_call | solution.py:237
  18.1 1.0 %split_basis.1 = (bf16[336,512]{1,0:T(8,128)(2,1)S(1)}, bf16[112,512]{1,0:T(8,128)(2,1)S(1)}) custom-call(bf16[448,512]{1,0:T(8,128)(2,1)} %source.1), custom_call_target="tpu_custom_call" | custom-call | tf_op jit(solution)/shard_map/split_basis/pallas_call | solution.py:282
  19.1 1.6 %collective-permute-start.15 = (bf16[336,512]{1,0:T(8,128)(2,1)S(1)}, bf16[336,512]{1,0:T(8,128)(2,1)S(1)}, u32[]{:S(2)}, u32[]{:S(2)}) collective-permute-start(bf16[336,512]{1,0:T(8,128)(2,1)S(1)} %get-tuple-element.25.refs_0_), channel_id=1, source_target_pairs={{0,2},{1,3},{2,0},{3,1},{4,6},{5,7},{6,4},{7,5},{8,10},{9,11},{10,... | collective-permute-start | bytes 1032200 | tf_op jit(solution)/shard_map/ppermute | solution.py:214
  20.7 2.1 %shard_map.74.refs_6_ = bf16[256,7168]{1,0:T(8,128)(2,1)S(1)} custom-call(s32[1]{0:T(128)} %bitcast.index_ref, bf16[256,7168]{1,0:T(8,128)(2,1)} %bitcast.6), custom_call_target="tpu_custom_call" | custom-call | tf_op jit(solution)/shard_map/pallas_call | solution.py:237
  22.8 2.2 %expert_work.1 = (bf16[4,16,1792]{2,1,0:T(8,128)(2,1)S(1)}, bf16[4,16,1792]{2,1,0:T(8,128)(2,1)S(1)}, bf16[4,16,1792]{2,1,0:T(8,128)(2,1)S(1)}, bf16[4,16,1792]{2,1,0:T(8,128)(2,1)S(1)}) custom-call(s32[1]{0:T(128)} %bitcast.index_ref, bf16[16,7168]{1,0:T(8,128)(2,1)S(1)} %stack_tokens.3.refs_0_, bf16[16,7168]{1,0:T(8,128)(2,1)S(1)} %stack_tokens.5.refs_1_, ...), custom_call_target="tpu_custom_call" | custom-call | tf_op jit(solution)/shard_map/expert_work/pallas_call | solution.py:297
  26.1 4.0 %collective-permute-done.15.refs_3_ = bf16[336,512]{1,0:T(8,128)(2,1)S(1)} collective-permute-done((bf16[336,512]{1,0:T(8,128)(2,1)S(1)}, bf16[336,512]{1,0:T(8,128)(2,1)S(1)}, u32[]{:S(2)}, u32[]{:S(2)}) %collective-permute-start.15) | collective-permute-done | bytes 344096 | tf_op jit(solution)/shard_map/ppermute | solution.py:214
  30.7 1.6 %collective-permute-start.11 = (bf16[2,16,1792]{2,1,0:T(8,128)(2,1)S(1)}, bf16[2,16,1792]{2,1,0:T(8,128)(2,1)S(1)}, u32[]{:S(2)}, u32[]{:S(2)}) collective-permute-start(bf16[2,16,1792]{2,1,0:T(8,128)(2,1)S(1)} %get-tuple-element.31), channel_id=1, source_target_pairs={{0,2},{1,3},{2,0},{3,1},{4,6},{5,7},{6,4},{7,5},{8,10},{9,11},{10,... | collective-permute-start | bytes 344072 | tf_op jit(solution)/shard_map/ppermute | solution.py:214
  32.3 1.3 %collective-permute-start.9 = (bf16[2,16,1792]{2,1,0:T(8,128)(2,1)S(1)}, bf16[2,16,1792]{2,1,0:T(8,128)(2,1)S(1)}, u32[]{:S(2)}, u32[]{:S(2)}) collective-permute-start(bf16[2,16,1792]{2,1,0:T(8,128)(2,1)S(1)} %get-tuple-element.32), channel_id=1, source_target_pairs={{0,2},{1,3},{2,0},{3,1},{4,6},{5,7},{6,4},{7,5},{8,10},{9,11},{10,... | collective-permute-start | bytes 344072 | tf_op jit(solution)/shard_map/ppermute | solution.py:214
  33.6 3.2 %collective-permute-done.11.crossed_ref = bf16[2,16,1792]{2,1,0:T(8,128)(2,1)S(1)} collective-permute-done((bf16[2,16,1792]{2,1,0:T(8,128)(2,1)S(1)}, bf16[2,16,1792]{2,1,0:T(8,128)(2,1)S(1)}, u32[]{:S(2)}, u32[]{:S(2)}) %collective-permute-start.11) | collective-permute-done | bytes 114720 | tf_op jit(solution)/shard_map/ppermute | solution.py:214
  36.8 1.3 %collective-permute-start.13 = (bf16[16,1792]{1,0:T(8,128)(2,1)S(1)}, bf16[16,1792]{1,0:T(8,128)(2,1)S(1)}, u32[]{:S(2)}, u32[]{:S(2)}) collective-permute-start(bf16[16,1792]{1,0:T(8,128)(2,1)S(1)} %shard_map.77), channel_id=1, source_target_pairs={{0,12},{1,13},{2,14},{3,15},{4,8},{5,9},{6,10},{7,11},{8,4},{9,5},... | collective-permute-start | bytes 172040 | tf_op jit(solution)/shard_map/ppermute | solution.py:214
  38.3 1.2 %collective-permute-start.12 = (bf16[16,1792]{1,0:T(8,128)(2,1)S(1)}, bf16[16,1792]{1,0:T(8,128)(2,1)S(1)}, u32[]{:S(2)}, u32[]{:S(2)}) collective-permute-start(bf16[16,1792]{1,0:T(8,128)(2,1)S(1)} %shard_map.76), channel_id=1, source_target_pairs={{0,8},{1,9},{2,10},{3,11},{4,12},{5,13},{6,14},{7,15},{8,0},{9,1},... | collective-permute-start | bytes 172040 | tf_op jit(solution)/shard_map/ppermute | solution.py:214
  39.5 2.0 %collective-permute-start.10 = (bf16[16,1792]{1,0:T(8,128)(2,1)S(1)}, bf16[16,1792]{1,0:T(8,128)(2,1)S(1)}, u32[]{:S(2)}, u32[]{:S(2)}) collective-permute-start(bf16[16,1792]{1,0:T(8,128)(2,1)S(1)} %shard_map.75), channel_id=1, source_target_pairs={{0,4},{1,5},{2,6},{3,7},{4,0},{5,1},{6,2},{7,3},{8,12},{9,13},{10,... | collective-permute-start | bytes 172040 | tf_op jit(solution)/shard_map/ppermute | solution.py:214
  41.6 1.9 %collective-permute-done.13.refs_2_ = bf16[16,1792]{1,0:T(8,128)(2,1)S(1)} collective-permute-done((bf16[16,1792]{1,0:T(8,128)(2,1)S(1)}, bf16[16,1792]{1,0:T(8,128)(2,1)S(1)}, u32[]{:S(2)}, u32[]{:S(2)}) %collective-permute-start.13) | collective-permute-done | bytes 57376 | tf_op jit(solution)/shard_map/ppermute | solution.py:214
  43.5 0.8 %collective-permute-done.12.refs_1_ = bf16[16,1792]{1,0:T(8,128)(2,1)S(1)} collective-permute-done((bf16[16,1792]{1,0:T(8,128)(2,1)S(1)}, bf16[16,1792]{1,0:T(8,128)(2,1)S(1)}, u32[]{:S(2)}, u32[]{:S(2)}) %collective-permute-start.12) | collective-permute-done | bytes 57376 | tf_op jit(solution)/shard_map/ppermute | solution.py:214
  44.9 1.2 %collective-permute-start.19 = (f32[8,512]{1,0:T(8,128)S(1)}, f32[8,512]{1,0:T(8,128)S(1)}, u32[]{:S(2)}, u32[]{:S(2)}) collective-permute-start(f32[8,512]{1,0:T(8,128)S(1)} %get-tuple-element.27), channel_id=1, source_target_pairs={{0,8},{1,9},{2,10},{3,11},{4,12},{5,13},{6,14},{7,15},{8,0},{9,1},... | collective-permute-start | bytes 49160 | tf_op jit(solution)/shard_map/ppermute | solution.py:214
  46.1 2.5 %collective-permute-start.20 = (f32[8,512]{1,0:T(8,128)S(1)}, f32[8,512]{1,0:T(8,128)S(1)}, u32[]{:S(2)}, u32[]{:S(2)}) collective-permute-start(f32[8,512]{1,0:T(8,128)S(1)} %get-tuple-element.28), channel_id=1, source_target_pairs={{0,12},{1,13},{2,14},{3,15},{4,8},{5,9},{6,10},{7,11},{8,4},{9,5},... | collective-permute-start | bytes 49160 | tf_op jit(solution)/shard_map/ppermute | solution.py:214
  48.6 0.9 %collective-permute-done.19 = f32[8,512]{1,0:T(8,128)S(1)} collective-permute-done((f32[8,512]{1,0:T(8,128)S(1)}, f32[8,512]{1,0:T(8,128)S(1)}, u32[]{:S(2)}, u32[]{:S(2)}) %collective-permute-start.19) | collective-permute-done | bytes 16416 | tf_op jit(solution)/shard_map/ppermute | solution.py:214
  49.6 2.0 %collective-permute-done.20 = f32[8,512]{1,0:T(8,128)S(1)} collective-permute-done((f32[8,512]{1,0:T(8,128)S(1)}, f32[8,512]{1,0:T(8,128)S(1)}, u32[]{:S(2)}, u32[]{:S(2)}) %collective-permute-start.20) | collective-permute-done | bytes 16416 | tf_op jit(solution)/shard_map/ppermute | solution.py:214
  51.6 0.7 %collective-permute-done.21 = f32[8,512]{1,0:T(8,128)S(1)} collective-permute-done((f32[8,512]{1,0:T(8,128)S(1)}, f32[8,512]{1,0:T(8,128)S(1)}, u32[]{:S(2)}, u32[]{:S(2)}) %collective-permute-start.21) | collective-permute-done | bytes 16416 | tf_op jit(solution)/shard_map/ppermute | solution.py:214
  (46 shorter events, 4.7 us)
Async XLA Ops:
  0.0 5.6 %collective-permute-start = (bf16[4,7168]{1,0:T(4,128)(2,1)}, bf16[4,7168]{1,0:T(4,128)(2,1)S(1)}, u32[]{:S(2)}, u32[]{:S(2)}) collective-permute-start(bf16[4,7168]{1,0:T(4,128)(2,1)} %refs_2_.1), channel_id=1, source_target_pairs={{0,4},{1,5},{2,6},{3,7},{4,0},{5,1},{6,2},{7,3},{8,12},{9,13},{10,... | collective-permute-start | bytes 172040 | tf_op jit(solution)/shard_map/ppermute | solution.py:214
  3.1 6.4 %collective-permute-start.1 = (bf16[4,7168]{1,0:T(4,128)(2,1)}, bf16[4,7168]{1,0:T(4,128)(2,1)S(1)}, u32[]{:S(2)}, u32[]{:S(2)}) collective-permute-start(bf16[4,7168]{1,0:T(4,128)(2,1)} %refs_2_.1), channel_id=1, source_target_pairs={{0,8},{1,9},{2,10},{3,11},{4,12},{5,13},{6,14},{7,15},{8,0},{9,1},... | collective-permute-start | bytes 172040 | tf_op jit(solution)/shard_map/ppermute | solution.py:214
  5.6 6.2 %collective-permute-start.2 = (bf16[4,7168]{1,0:T(4,128)(2,1)}, bf16[4,7168]{1,0:T(4,128)(2,1)S(1)}, u32[]{:S(2)}, u32[]{:S(2)}) collective-permute-start(bf16[4,7168]{1,0:T(4,128)(2,1)} %refs_2_.1), channel_id=1, source_target_pairs={{0,12},{1,13},{2,14},{3,15},{4,8},{5,9},{6,10},{7,11},{8,4},{9,5},... | collective-permute-start | bytes 172040 | tf_op jit(solution)/shard_map/ppermute | solution.py:214
  11.8 6.1 %collective-permute-start.4 = (bf16[3,4,7168]{2,1,0:T(4,128)(2,1)S(1)}, bf16[3,4,7168]{2,1,0:T(4,128)(2,1)S(1)}, u32[]{:S(2)}, u32[]{:S(2)}) collective-permute-start(bf16[3,4,7168]{2,1,0:T(4,128)(2,1)S(1)} %stack_tokens.4), channel_id=1, source_target_pairs={{0,2},{1,3},{2,0},{3,1},{4,6},{5,7},{6,4},{7,5},{8,10},{9,11},{10,... | collective-permute-start | bytes 516104 | tf_op jit(solution)/shard_map/ppermute | solution.py:214
  13.4 4.5 %collective-permute-start.3 = (bf16[4,7168]{1,0:T(4,128)(2,1)}, bf16[4,7168]{1,0:T(4,128)(2,1)S(1)}, u32[]{:S(2)}, u32[]{:S(2)}) collective-permute-start(bf16[4,7168]{1,0:T(4,128)(2,1)} %refs_2_.1), channel_id=1, source_target_pairs={{0,2},{1,3},{2,0},{3,1},{4,6},{5,7},{6,4},{7,5},{8,10},{9,11},{10,... | collective-permute-start | bytes 172040 | tf_op jit(solution)/shard_map/ppermute | solution.py:214
  17.2 5.5 %collective-permute-start.5 = (bf16[16,7168]{1,0:T(8,128)(2,1)S(1)}, bf16[16,7168]{1,0:T(8,128)(2,1)S(1)}, u32[]{:S(2)}, u32[]{:S(2)}) collective-permute-start(bf16[16,7168]{1,0:T(8,128)(2,1)S(1)} %stack_tokens.3.refs_0_), channel_id=1, source_target_pairs={{0,1},{1,0},{2,3},{3,2},{4,5},{5,4},{6,7},{7,6},{8,9},{9,8},{10,11... | collective-permute-start | bytes 688136 | tf_op jit(solution)/shard_map/ppermute | solution.py:214
  18.0 4.8 %collective-permute-start.6 = (bf16[16,7168]{1,0:T(8,128)(2,1)S(1)}, bf16[16,7168]{1,0:T(8,128)(2,1)S(1)}, u32[]{:S(2)}, u32[]{:S(2)}) collective-permute-start(bf16[16,7168]{1,0:T(8,128)(2,1)S(1)} %stack_tokens.5.refs_1_), channel_id=1, source_target_pairs={{0,1},{1,0},{2,3},{3,2},{4,5},{5,4},{6,7},{7,6},{8,9},{9,8},{10,11... | collective-permute-start | bytes 688136 | tf_op jit(solution)/shard_map/ppermute | solution.py:214
  19.1 11.0 %collective-permute-start.15 = (bf16[336,512]{1,0:T(8,128)(2,1)S(1)}, bf16[336,512]{1,0:T(8,128)(2,1)S(1)}, u32[]{:S(2)}, u32[]{:S(2)}) collective-permute-start(bf16[336,512]{1,0:T(8,128)(2,1)S(1)} %get-tuple-element.25.refs_0_), channel_id=1, source_target_pairs={{0,2},{1,3},{2,0},{3,1},{4,6},{5,7},{6,4},{7,5},{8,10},{9,11},{10,... | collective-permute-start | bytes 1032200 | tf_op jit(solution)/shard_map/ppermute | solution.py:214
  22.8 10.8 %copy-start.2 = (s32[4,2]{0,1:T(2,128)S(1)}, s32[4,2]{0,1:T(2,128)}, u32[]{:S(2)}) copy-start(s32[4,2]{0,1:T(2,128)} %param.9) | copy-start | bytes 100
  25.0 5.6 %collective-permute-start.8 = (bf16[4,16,1792]{2,1,0:T(8,128)(2,1)S(1)}, bf16[4,16,1792]{2,1,0:T(8,128)(2,1)S(1)}, u32[]{:S(2)}, u32[]{:S(2)}) collective-permute-start(bf16[4,16,1792]{2,1,0:T(8,128)(2,1)S(1)} %get-tuple-element.24), channel_id=1, source_target_pairs={{0,1},{1,0},{2,3},{3,2},{4,5},{5,4},{6,7},{7,6},{8,9},{9,8},{10,11... | collective-permute-start | bytes 688136 | tf_op jit(solution)/shard_map/ppermute | solution.py:214
  25.3 16.2 %collective-permute-start.14 = (bf16[448,512]{1,0:T(8,128)(2,1)S(1)}, bf16[448,512]{1,0:T(8,128)(2,1)S(1)}, u32[]{:S(2)}, u32[]{:S(2)}) collective-permute-start(bf16[448,512]{1,0:T(8,128)(2,1)S(1)} %copy-done), channel_id=1, source_target_pairs={{0,1},{1,0},{2,3},{3,2},{4,5},{5,4},{6,7},{7,6},{8,9},{9,8},{10,11... | collective-permute-start | bytes 1376264 | tf_op jit(solution)/shard_map/ppermute | solution.py:214
  25.6 6.7 %collective-permute-start.16 = (bf16[112,512]{1,0:T(8,128)(2,1)S(1)}, bf16[112,512]{1,0:T(8,128)(2,1)S(1)}, u32[]{:S(2)}, u32[]{:S(2)}) collective-permute-start(bf16[112,512]{1,0:T(8,128)(2,1)S(1)} %get-tuple-element.26.refs_1_), channel_id=1, source_target_pairs={{0,2},{1,3},{2,0},{3,1},{4,6},{5,7},{6,4},{7,5},{8,10},{9,11},{10,... | collective-permute-start | bytes 344072 | tf_op jit(solution)/shard_map/ppermute | solution.py:214
  30.1 11.4 %collective-permute-start.17 = (bf16[336,512]{1,0:T(8,128)(2,1)S(1)}, bf16[336,512]{1,0:T(8,128)(2,1)S(1)}, u32[]{:S(2)}, u32[]{:S(2)}) collective-permute-start(bf16[336,512]{1,0:T(8,128)(2,1)S(1)} %collective-permute-done.15.refs_3_), channel_id=1, source_target_pairs={{0,1},{1,0},{2,3},{3,2},{4,5},{5,4},{6,7},{7,6},{8,9},{9,8},{10,11... | collective-permute-start | bytes 1032200 | tf_op jit(solution)/shard_map/ppermute | solution.py:214
  30.1 3.5 %collective-permute-start.7 = (bf16[4,16,1792]{2,1,0:T(8,128)(2,1)S(1)}, bf16[4,16,1792]{2,1,0:T(8,128)(2,1)S(1)}, u32[]{:S(2)}, u32[]{:S(2)}) collective-permute-start(bf16[4,16,1792]{2,1,0:T(8,128)(2,1)S(1)} %get-tuple-element.22), channel_id=1, source_target_pairs={{0,1},{1,0},{2,3},{3,2},{4,5},{5,4},{6,7},{7,6},{8,9},{9,8},{10,11... | collective-permute-start | bytes 688136 | tf_op jit(solution)/shard_map/ppermute | solution.py:214
  30.7 6.1 %collective-permute-start.11 = (bf16[2,16,1792]{2,1,0:T(8,128)(2,1)S(1)}, bf16[2,16,1792]{2,1,0:T(8,128)(2,1)S(1)}, u32[]{:S(2)}, u32[]{:S(2)}) collective-permute-start(bf16[2,16,1792]{2,1,0:T(8,128)(2,1)S(1)} %get-tuple-element.31), channel_id=1, source_target_pairs={{0,2},{1,3},{2,0},{3,1},{4,6},{5,7},{6,4},{7,5},{8,10},{9,11},{10,... | collective-permute-start | bytes 344072 | tf_op jit(solution)/shard_map/ppermute | solution.py:214
  32.3 6.0 %collective-permute-start.9 = (bf16[2,16,1792]{2,1,0:T(8,128)(2,1)S(1)}, bf16[2,16,1792]{2,1,0:T(8,128)(2,1)S(1)}, u32[]{:S(2)}, u32[]{:S(2)}) collective-permute-start(bf16[2,16,1792]{2,1,0:T(8,128)(2,1)S(1)} %get-tuple-element.32), channel_id=1, source_target_pairs={{0,2},{1,3},{2,0},{3,1},{4,6},{5,7},{6,4},{7,5},{8,10},{9,11},{10,... | collective-permute-start | bytes 344072 | tf_op jit(solution)/shard_map/ppermute | solution.py:214
  33.6 5.9 %collective-permute-start.18 = (bf16[112,512]{1,0:T(8,128)(2,1)S(1)}, bf16[112,512]{1,0:T(8,128)(2,1)S(1)}, u32[]{:S(2)}, u32[]{:S(2)}) collective-permute-start(bf16[112,512]{1,0:T(8,128)(2,1)S(1)} %collective-permute-done.16.refs_4_), channel_id=1, source_target_pairs={{0,1},{1,0},{2,3},{3,2},{4,5},{5,4},{6,7},{7,6},{8,9},{9,8},{10,11... | collective-permute-start | bytes 344072 | tf_op jit(solution)/shard_map/ppermute | solution.py:214
  36.8 11.8 %copy-start.1 = (s32[4,2]{0,1:T(2,128)S(1)}, s32[4,2]{0,1:T(2,128)}, u32[]{:S(2)}) copy-start(s32[4,2]{0,1:T(2,128)} %param.8) | copy-start | bytes 100
  36.8 6.7 %collective-permute-start.13 = (bf16[16,1792]{1,0:T(8,128)(2,1)S(1)}, bf16[16,1792]{1,0:T(8,128)(2,1)S(1)}, u32[]{:S(2)}, u32[]{:S(2)}) collective-permute-start(bf16[16,1792]{1,0:T(8,128)(2,1)S(1)} %shard_map.77), channel_id=1, source_target_pairs={{0,12},{1,13},{2,14},{3,15},{4,8},{5,9},{6,10},{7,11},{8,4},{9,5},... | collective-permute-start | bytes 172040 | tf_op jit(solution)/shard_map/ppermute | solution.py:214
  38.3 6.1 %collective-permute-start.12 = (bf16[16,1792]{1,0:T(8,128)(2,1)S(1)}, bf16[16,1792]{1,0:T(8,128)(2,1)S(1)}, u32[]{:S(2)}, u32[]{:S(2)}) collective-permute-start(bf16[16,1792]{1,0:T(8,128)(2,1)S(1)} %shard_map.76), channel_id=1, source_target_pairs={{0,8},{1,9},{2,10},{3,11},{4,12},{5,13},{6,14},{7,15},{8,0},{9,1},... | collective-permute-start | bytes 172040 | tf_op jit(solution)/shard_map/ppermute | solution.py:214
  39.5 4.9 %collective-permute-start.10 = (bf16[16,1792]{1,0:T(8,128)(2,1)S(1)}, bf16[16,1792]{1,0:T(8,128)(2,1)S(1)}, u32[]{:S(2)}, u32[]{:S(2)}) collective-permute-start(bf16[16,1792]{1,0:T(8,128)(2,1)S(1)} %shard_map.75), channel_id=1, source_target_pairs={{0,4},{1,5},{2,6},{3,7},{4,0},{5,1},{6,2},{7,3},{8,12},{9,13},{10,... | collective-permute-start | bytes 172040 | tf_op jit(solution)/shard_map/ppermute | solution.py:214
  44.9 4.7 %collective-permute-start.19 = (f32[8,512]{1,0:T(8,128)S(1)}, f32[8,512]{1,0:T(8,128)S(1)}, u32[]{:S(2)}, u32[]{:S(2)}) collective-permute-start(f32[8,512]{1,0:T(8,128)S(1)} %get-tuple-element.27), channel_id=1, source_target_pairs={{0,8},{1,9},{2,10},{3,11},{4,12},{5,13},{6,14},{7,15},{8,0},{9,1},... | collective-permute-start | bytes 49160 | tf_op jit(solution)/shard_map/ppermute | solution.py:214
  46.1 5.5 %collective-permute-start.20 = (f32[8,512]{1,0:T(8,128)S(1)}, f32[8,512]{1,0:T(8,128)S(1)}, u32[]{:S(2)}, u32[]{:S(2)}) collective-permute-start(f32[8,512]{1,0:T(8,128)S(1)} %get-tuple-element.28), channel_id=1, source_target_pairs={{0,12},{1,13},{2,14},{3,15},{4,8},{5,9},{6,10},{7,11},{8,4},{9,5},... | collective-permute-start | bytes 49160 | tf_op jit(solution)/shard_map/ppermute | solution.py:214
  48.6 3.7 %collective-permute-start.21 = (f32[8,512]{1,0:T(8,128)S(1)}, f32[8,512]{1,0:T(8,128)S(1)}, u32[]{:S(2)}, u32[]{:S(2)}) collective-permute-start(f32[8,512]{1,0:T(8,128)S(1)} %get-tuple-element.29), channel_id=1, source_target_pairs={{0,4},{1,5},{2,6},{3,7},{4,0},{5,1},{6,2},{7,3},{8,12},{9,13},{10,... | collective-permute-start | bytes 49160 | tf_op jit(solution)/shard_map/ppermute | solution.py:214
  (1 other events, 2.5 us)

commit v2 on v1

--- a/solution.py
+++ b/solution.py
@@ -70,29 +70,17 @@
     return jnp.sum(weights[:, :, None] * projected, axis=1).astype(jnp.bfloat16)
 
 
-def fetch_kernel(parts, index_ref, *refs):
+def fetch_kernel(plan, index_ref, *refs):
     del index_ref
-    sources, targets, sems = refs[: len(parts)], refs[len(parts) : -1], refs[-1]
+    sources, targets, sems = refs[: -len(plan) - 1], refs[-len(plan) - 1 : -1], refs[-1]
     copies = []
-    for source, target, count in zip(sources, targets, parts):
+    for (operand, first, count), target in zip(plan, targets):
         rows = target.shape[0] // count
         for k in range(count):
-            block = pl.ds(k * rows, rows)
+            source = sources[operand].at[pl.ds(first + k * rows, rows), :]
             sem = sems.at[len(copies)]
-            copies.append(pltpu.make_async_copy(source.at[block, :], target.at[block, :], sem))
+            copies.append(pltpu.make_async_copy(source, target.at[pl.ds(k * rows, rows), :], sem))
             copies[-1].start()
-    for copy in copies:
-        copy.wait()
-
-
-def split_kernel(source, *refs):
-    targets, sems = refs[:-1], refs[-1]
-    copies, at = [], 0
-    for n, target in enumerate(targets):
-        rows = target.shape[0]
-        copies.append(pltpu.make_async_copy(source.at[pl.ds(at, rows), :], target, sems.at[n]))
-        copies[n].start()
-        at += rows
     for copy in copies:
         copy.wait()
 
@@ -232,20 +220,36 @@
 
     hbm = pl.BlockSpec(memory_space=pltpu.HBM)
 
-    def fetch(parts, *operands):
+    def fetch(operands, plan):
         operands = [pltpu.with_memory_space_constraint(x, pltpu.HBM) for x in operands]
+        targets = [
+            pltpu.VMEM((count, operands[operand].shape[1]), operands[operand].dtype)
+            for operand, _, count, _ in plan
+        ]
+        copies = [(operand, first, count) for operand, first, _, count in plan]
         out = pl.pallas_call(
-            functools.partial(fetch_kernel, parts),
-            out_shape=tuple(pltpu.VMEM(x.shape, x.dtype) for x in operands),
+            functools.partial(fetch_kernel, copies),
+            out_shape=tuple(targets),
             in_specs=[smem] + [hbm] * len(operands),
-            out_specs=(vmem,) * len(operands),
-            scratch_shapes=[pltpu.SemaphoreType.DMA((sum(parts),))],
+            out_specs=(vmem,) * len(plan),
+            scratch_shapes=[pltpu.SemaphoreType.DMA((sum(count for *_, count in plan),))],
             compiler_params=pltpu.CompilerParams(vmem_limit_bytes=MIB),
         )(index, *operands)
         return [pltpu.with_memory_space_constraint(x, pltpu.VMEM) for x in out]
 
-    gate, up, own = fetch((FETCH_PARTS, FETCH_PARTS, 1), gate_weight[0], up_weight[0], tokens)
-    (down,) = fetch((FETCH_PARTS,), down_weight[0])
+    shard = target_basis.shape[0]
+    late = shard // 64 * 16
+    gate, up, own, *basis_parts = fetch(
+        (gate_weight[0], up_weight[0], tokens, target_basis),
+        (
+            (0, 0, width, FETCH_PARTS),
+            (1, 0, width, FETCH_PARTS),
+            (2, 0, rows, 1),
+            (3, 0, shard - late, 1),
+            (3, shard - late, late, 1),
+        ),
+    )
+    (down,) = fetch((down_weight[0],), ((0, 0, down_weight.shape[1], FETCH_PARTS),))
 
     def stack(kernel, shape, blocks):
         return pl.pallas_call(
@@ -277,17 +281,6 @@
     ]
     stacks += [core_swap(tokens_stack) for tokens_stack in stacks]
 
-    shard = target_basis.shape[0]
-    late = shard // 64 * 16
-    basis_parts = pl.pallas_call(
-        split_kernel,
-        out_shape=tuple(pltpu.VMEM((n, rank), bf16) for n in (shard - late, late)),
-        in_specs=[hbm],
-        out_specs=(vmem,) * 2,
-        scratch_shapes=[pltpu.SemaphoreType.DMA((2,))],
-        compiler_params=pltpu.CompilerParams(vmem_limit_bytes=MIB),
-        name="split_basis",
-    )(pltpu.with_memory_space_constraint(target_basis, pltpu.HBM))
     column_parts = [column_swap(x) for x in basis_parts]
     basis_shards = [
         *basis_parts, core_swap(target_basis), *column_parts, *[core_swap(x) for x in column_parts]

time: 53.2 us -> 52.2 us (0.981)
  Pallas kernels: 9.37 us -> 8.49 us
    pallas_call x3 -> x2, Pallas kernels: 6.3 us -> 5.41 us  [fetch(): pl.pallas_call(functools.partial(fetch_kernel, copies), out_shape=tuple(t...]
  transfers between devices with their start and end apart: 22 -> 22, of which waited for: 11 -> 11; matrix products, arithmetic and copies ran while one was open for 0% -> 0% of each run, Pallas kernels for 17% -> 15%
where the time goes in v2:
time: 52.2 us; the launch traced here: 52 us
  starting transfers between devices  22.1 us (42%)
  waiting for transfers between devices  20.4 us (39%)
  Pallas kernels  8.49 us (16%)
  other arithmetic  0.78 us (1%)
    ppermute x22, starting transfers between devices, swap(): return lax.ppermute(x, 'expert', [(i, i ^ step) for i in range(devices)])  22.1 us
    ppermute x22, waiting for transfers between devices, swap(): return lax.ppermute(x, 'expert', [(i, i ^ step) for i in range(devices)])  20.4 us
    pallas_call x2, Pallas kernels, fetch(): pl.pallas_call(functools.partial(fetch_kernel, copies), out_shape=tuple(t...  5.41 us
    pallas_call x1, Pallas kernels, sharded_basis_shards(): pl.pallas_call(functools.partial(expert_kernel, order), out_shape=(piece,...  2.24 us
  transfers between devices with their start and end apart: 22, of which 11 were waited for; matrix products, arithmetic and copies ran while one was open for 0% of the time, Pallas kernels for 15%

profile of v2, /device:TPU:0, one launch (start us, length us, event | category | flops | bytes accessed | tf_op | source)
XLA Modules:
  0.0 52.0 jit_solution(15988298172344463966)
XLA Ops:
  0.0 3.1 %collective-permute-start = (bf16[4,7168]{1,0:T(4,128)(2,1)}, bf16[4,7168]{1,0:T(4,128)(2,1)S(1)}, u32[]{:S(2)}, u32[]{:S(2)}) collective-permute-start(bf16[4,7168]{1,0:T(4,128)(2,1)} %refs_2_.1), channel_id=1, source_target_pairs={{0,4},{1,5},{2,6},{3,7},{4,0},{5,1},{6,2},{7,3},{8,12},{9,13},{10,... | collective-permute-start | bytes 172040 | tf_op jit(solution)/shard_map/ppermute | solution.py:202
  3.1 2.6 %collective-permute-start.1 = (bf16[4,7168]{1,0:T(4,128)(2,1)}, bf16[4,7168]{1,0:T(4,128)(2,1)S(1)}, u32[]{:S(2)}, u32[]{:S(2)}) collective-permute-start(bf16[4,7168]{1,0:T(4,128)(2,1)} %refs_2_.1), channel_id=1, source_target_pairs={{0,8},{1,9},{2,10},{3,11},{4,12},{5,13},{6,14},{7,15},{8,0},{9,1},... | collective-permute-start | bytes 172040 | tf_op jit(solution)/shard_map/ppermute | solution.py:202
  5.6 3.8 %collective-permute-done.1.refs_2_.refs_1_ = bf16[4,7168]{1,0:T(4,128)(2,1)S(1)} collective-permute-done((bf16[4,7168]{1,0:T(4,128)(2,1)}, bf16[4,7168]{1,0:T(4,128)(2,1)S(1)}, u32[]{:S(2)}, u32[]{:S(2)}) %collective-permute-start.1) | collective-permute-done | bytes 57376 | tf_op jit(solution)/shard_map/ppermute | solution.py:202
  9.5 2.4 %collective-permute-done.2.refs_3_.refs_2_ = bf16[4,7168]{1,0:T(4,128)(2,1)S(1)} collective-permute-done((bf16[4,7168]{1,0:T(4,128)(2,1)}, bf16[4,7168]{1,0:T(4,128)(2,1)S(1)}, u32[]{:S(2)}, u32[]{:S(2)}) %collective-permute-start.2) | collective-permute-done | bytes 57376 | tf_op jit(solution)/shard_map/ppermute | solution.py:202
  11.8 1.6 %collective-permute-start.4 = (bf16[3,4,7168]{2,1,0:T(4,128)(2,1)S(1)}, bf16[3,4,7168]{2,1,0:T(4,128)(2,1)S(1)}, u32[]{:S(2)}, u32[]{:S(2)}) collective-permute-start(bf16[3,4,7168]{2,1,0:T(4,128)(2,1)S(1)} %stack_tokens.4), channel_id=1, source_target_pairs={{0,2},{1,3},{2,0},{3,1},{4,6},{5,7},{6,4},{7,5},{8,10},{9,11},{10,... | collective-permute-start | bytes 516104 | tf_op jit(solution)/shard_map/ppermute | solution.py:202
  13.9 3.4 %shard_map.73 = (bf16[7168,256]{1,0:T(8,128)(2,1)S(1)}, bf16[7168,256]{1,0:T(8,128)(2,1)S(1)}, bf16[4,7168]{1,0:T(4,128)(2,1)S(1)}, bf16[336,512]{1,0:T(8,128)(2,1)S(1)}, bf16[112,512]{1,0:T(8,128)(2,1)S(1)}) custom-call(s32[1]{0:T(128)} %bitcast.index_ref, bf16[7168,256]{1,0:T(8,128)(2,1)} %bitcast.4, bf16[7168,256]{1,0:T(8,128)(2,1)} %bitcast.5, ...), custom_call_target="tpu_custom_call" | custom-call | tf_op jit(solution)/shard_map/pallas_call | solution.py:230
  18.1 1.6 %collective-permute-start.15 = (bf16[336,512]{1,0:T(8,128)(2,1)S(1)}, bf16[336,512]{1,0:T(8,128)(2,1)S(1)}, u32[]{:S(2)}, u32[]{:S(2)}) collective-permute-start(bf16[336,512]{1,0:T(8,128)(2,1)S(1)} %get-tuple-element.25.refs_0_), channel_id=1, source_target_pairs={{0,2},{1,3},{2,0},{3,1},{4,6},{5,7},{6,4},{7,5},{8,10},{9,11},{10,... | collective-permute-start | bytes 1032200 | tf_op jit(solution)/shard_map/ppermute | solution.py:202
  19.7 2.1 %shard_map.74.refs_6_ = bf16[256,7168]{1,0:T(8,128)(2,1)S(1)} custom-call(s32[1]{0:T(128)} %bitcast.index_ref, bf16[256,7168]{1,0:T(8,128)(2,1)} %bitcast.6), custom_call_target="tpu_custom_call" | custom-call | tf_op jit(solution)/shard_map/pallas_call | solution.py:230
  21.8 2.2 %expert_work.1 = (bf16[4,16,1792]{2,1,0:T(8,128)(2,1)S(1)}, bf16[4,16,1792]{2,1,0:T(8,128)(2,1)S(1)}, bf16[4,16,1792]{2,1,0:T(8,128)(2,1)S(1)}, bf16[4,16,1792]{2,1,0:T(8,128)(2,1)S(1)}) custom-call(s32[1]{0:T(128)} %bitcast.index_ref, bf16[16,7168]{1,0:T(8,128)(2,1)S(1)} %stack_tokens.3.refs_0_, bf16[16,7168]{1,0:T(8,128)(2,1)S(1)} %stack_tokens.5.refs_1_, ...), custom_call_target="tpu_custom_call" | custom-call | tf_op jit(solution)/shard_map/expert_work/pallas_call | solution.py:290
  25.1 4.0 %collective-permute-done.15.refs_3_ = bf16[336,512]{1,0:T(8,128)(2,1)S(1)} collective-permute-done((bf16[336,512]{1,0:T(8,128)(2,1)S(1)}, bf16[336,512]{1,0:T(8,128)(2,1)S(1)}, u32[]{:S(2)}, u32[]{:S(2)}) %collective-permute-start.15) | collective-permute-done | bytes 344096 | tf_op jit(solution)/shard_map/ppermute | solution.py:202
  29.7 1.6 %collective-permute-start.11 = (bf16[2,16,1792]{2,1,0:T(8,128)(2,1)S(1)}, bf16[2,16,1792]{2,1,0:T(8,128)(2,1)S(1)}, u32[]{:S(2)}, u32[]{:S(2)}) collective-permute-start(bf16[2,16,1792]{2,1,0:T(8,128)(2,1)S(1)} %get-tuple-element.31), channel_id=1, source_target_pairs={{0,2},{1,3},{2,0},{3,1},{4,6},{5,7},{6,4},{7,5},{8,10},{9,11},{10,... | collective-permute-start | bytes 344072 | tf_op jit(solution)/shard_map/ppermute | solution.py:202
  31.3 1.3 %collective-permute-start.9 = (bf16[2,16,1792]{2,1,0:T(8,128)(2,1)S(1)}, bf16[2,16,1792]{2,1,0:T(8,128)(2,1)S(1)}, u32[]{:S(2)}, u32[]{:S(2)}) collective-permute-start(bf16[2,16,1792]{2,1,0:T(8,128)(2,1)S(1)} %get-tuple-element.32), channel_id=1, source_target_pairs={{0,2},{1,3},{2,0},{3,1},{4,6},{5,7},{6,4},{7,5},{8,10},{9,11},{10,... | collective-permute-start | bytes 344072 | tf_op jit(solution)/shard_map/ppermute | solution.py:202
  32.6 3.2 %collective-permute-done.11.crossed_ref = bf16[2,16,1792]{2,1,0:T(8,128)(2,1)S(1)} collective-permute-done((bf16[2,16,1792]{2,1,0:T(8,128)(2,1)S(1)}, bf16[2,16,1792]{2,1,0:T(8,128)(2,1)S(1)}, u32[]{:S(2)}, u32[]{:S(2)}) %collective-permute-start.11) | collective-permute-done | bytes 114720 | tf_op jit(solution)/shard_map/ppermute | solution.py:202
  35.8 1.3 %collective-permute-start.13 = (bf16[16,1792]{1,0:T(8,128)(2,1)S(1)}, bf16[16,1792]{1,0:T(8,128)(2,1)S(1)}, u32[]{:S(2)}, u32[]{:S(2)}) collective-permute-start(bf16[16,1792]{1,0:T(8,128)(2,1)S(1)} %shard_map.77), channel_id=1, source_target_pairs={{0,12},{1,13},{2,14},{3,15},{4,8},{5,9},{6,10},{7,11},{8,4},{9,5},... | collective-permute-start | bytes 172040 | tf_op jit(solution)/shard_map/ppermute | solution.py:202
  37.3 1.2 %collective-permute-start.12 = (bf16[16,1792]{1,0:T(8,128)(2,1)S(1)}, bf16[16,1792]{1,0:T(8,128)(2,1)S(1)}, u32[]{:S(2)}, u32[]{:S(2)}) collective-permute-start(bf16[16,1792]{1,0:T(8,128)(2,1)S(1)} %shard_map.76), channel_id=1, source_target_pairs={{0,8},{1,9},{2,10},{3,11},{4,12},{5,13},{6,14},{7,15},{8,0},{9,1},... | collective-permute-start | bytes 172040 | tf_op jit(solution)/shard_map/ppermute | solution.py:202
  38.5 2.0 %collective-permute-start.10 = (bf16[16,1792]{1,0:T(8,128)(2,1)S(1)}, bf16[16,1792]{1,0:T(8,128)(2,1)S(1)}, u32[]{:S(2)}, u32[]{:S(2)}) collective-permute-start(bf16[16,1792]{1,0:T(8,128)(2,1)S(1)} %shard_map.75), channel_id=1, source_target_pairs={{0,4},{1,5},{2,6},{3,7},{4,0},{5,1},{6,2},{7,3},{8,12},{9,13},{10,... | collective-permute-start | bytes 172040 | tf_op jit(solution)/shard_map/ppermute | solution.py:202
  40.6 1.9 %collective-permute-done.13.refs_2_ = bf16[16,1792]{1,0:T(8,128)(2,1)S(1)} collective-permute-done((bf16[16,1792]{1,0:T(8,128)(2,1)S(1)}, bf16[16,1792]{1,0:T(8,128)(2,1)S(1)}, u32[]{:S(2)}, u32[]{:S(2)}) %collective-permute-start.13) | collective-permute-done | bytes 57376 | tf_op jit(solution)/shard_map/ppermute | solution.py:202
  42.5 0.8 %collective-permute-done.12.refs_1_ = bf16[16,1792]{1,0:T(8,128)(2,1)S(1)} collective-permute-done((bf16[16,1792]{1,0:T(8,128)(2,1)S(1)}, bf16[16,1792]{1,0:T(8,128)(2,1)S(1)}, u32[]{:S(2)}, u32[]{:S(2)}) %collective-permute-start.12) | collective-permute-done | bytes 57376 | tf_op jit(solution)/shard_map/ppermute | solution.py:202
  43.8 1.2 %collective-permute-start.19 = (f32[8,512]{1,0:T(8,128)S(1)}, f32[8,512]{1,0:T(8,128)S(1)}, u32[]{:S(2)}, u32[]{:S(2)}) collective-permute-start(f32[8,512]{1,0:T(8,128)S(1)} %get-tuple-element.27), channel_id=1, source_target_pairs={{0,8},{1,9},{2,10},{3,11},{4,12},{5,13},{6,14},{7,15},{8,0},{9,1},... | collective-permute-start | bytes 49160 | tf_op jit(solution)/shard_map/ppermute | solution.py:202
  45.0 2.5 %collective-permute-start.20 = (f32[8,512]{1,0:T(8,128)S(1)}, f32[8,512]{1,0:T(8,128)S(1)}, u32[]{:S(2)}, u32[]{:S(2)}) collective-permute-start(f32[8,512]{1,0:T(8,128)S(1)} %get-tuple-element.28), channel_id=1, source_target_pairs={{0,12},{1,13},{2,14},{3,15},{4,8},{5,9},{6,10},{7,11},{8,4},{9,5},... | collective-permute-start | bytes 49160 | tf_op jit(solution)/shard_map/ppermute | solution.py:202
  47.6 0.9 %collective-permute-done.19 = f32[8,512]{1,0:T(8,128)S(1)} collective-permute-done((f32[8,512]{1,0:T(8,128)S(1)}, f32[8,512]{1,0:T(8,128)S(1)}, u32[]{:S(2)}, u32[]{:S(2)}) %collective-permute-start.19) | collective-permute-done | bytes 16416 | tf_op jit(solution)/shard_map/ppermute | solution.py:202
  48.5 2.0 %collective-permute-done.20 = f32[8,512]{1,0:T(8,128)S(1)} collective-permute-done((f32[8,512]{1,0:T(8,128)S(1)}, f32[8,512]{1,0:T(8,128)S(1)}, u32[]{:S(2)}, u32[]{:S(2)}) %collective-permute-start.20) | collective-permute-done | bytes 16416 | tf_op jit(solution)/shard_map/ppermute | solution.py:202
  50.6 0.7 %collective-permute-done.21 = f32[8,512]{1,0:T(8,128)S(1)} collective-permute-done((f32[8,512]{1,0:T(8,128)S(1)}, f32[8,512]{1,0:T(8,128)S(1)}, u32[]{:S(2)}, u32[]{:S(2)}) %collective-permute-start.21) | collective-permute-done | bytes 16416 | tf_op jit(solution)/shard_map/ppermute | solution.py:202
  51.3 0.7 %multiply_reduce_fusion = bf16[4,512]{1,0:T(4,128)(2,1)} fusion(f32[2,4,512]{2,1,0:T(4,128)S(1)} %reshape.11, f32[2,4]{1,0:T(2,128)S(1)} %fusion), kind=kLoop, calls=%fused_computation.1 | loop fusion | flops 6144 | bytes 20512 | tf_op jit(solution)/shard_map/reduce_sum | solution.py:344
  (45 shorter events, 3.9 us)
Async XLA Ops:
  0.0 5.6 %collective-permute-start = (bf16[4,7168]{1,0:T(4,128)(2,1)}, bf16[4,7168]{1,0:T(4,128)(2,1)S(1)}, u32[]{:S(2)}, u32[]{:S(2)}) collective-permute-start(bf16[4,7168]{1,0:T(4,128)(2,1)} %refs_2_.1), channel_id=1, source_target_pairs={{0,4},{1,5},{2,6},{3,7},{4,0},{5,1},{6,2},{7,3},{8,12},{9,13},{10,... | collective-permute-start | bytes 172040 | tf_op jit(solution)/shard_map/ppermute | solution.py:202
  3.1 6.4 %collective-permute-start.1 = (bf16[4,7168]{1,0:T(4,128)(2,1)}, bf16[4,7168]{1,0:T(4,128)(2,1)S(1)}, u32[]{:S(2)}, u32[]{:S(2)}) collective-permute-start(bf16[4,7168]{1,0:T(4,128)(2,1)} %refs_2_.1), channel_id=1, source_target_pairs={{0,8},{1,9},{2,10},{3,11},{4,12},{5,13},{6,14},{7,15},{8,0},{9,1},... | collective-permute-start | bytes 172040 | tf_op jit(solution)/shard_map/ppermute | solution.py:202
  5.6 6.2 %collective-permute-start.2 = (bf16[4,7168]{1,0:T(4,128)(2,1)}, bf16[4,7168]{1,0:T(4,128)(2,1)S(1)}, u32[]{:S(2)}, u32[]{:S(2)}) collective-permute-start(bf16[4,7168]{1,0:T(4,128)(2,1)} %refs_2_.1), channel_id=1, source_target_pairs={{0,12},{1,13},{2,14},{3,15},{4,8},{5,9},{6,10},{7,11},{8,4},{9,5},... | collective-permute-start | bytes 172040 | tf_op jit(solution)/shard_map/ppermute | solution.py:202
  11.8 6.1 %collective-permute-start.4 = (bf16[3,4,7168]{2,1,0:T(4,128)(2,1)S(1)}, bf16[3,4,7168]{2,1,0:T(4,128)(2,1)S(1)}, u32[]{:S(2)}, u32[]{:S(2)}) collective-permute-start(bf16[3,4,7168]{2,1,0:T(4,128)(2,1)S(1)} %stack_tokens.4), channel_id=1, source_target_pairs={{0,2},{1,3},{2,0},{3,1},{4,6},{5,7},{6,4},{7,5},{8,10},{9,11},{10,... | collective-permute-start | bytes 516104 | tf_op jit(solution)/shard_map/ppermute | solution.py:202
  13.4 4.5 %collective-permute-start.3 = (bf16[4,7168]{1,0:T(4,128)(2,1)}, bf16[4,7168]{1,0:T(4,128)(2,1)S(1)}, u32[]{:S(2)}, u32[]{:S(2)}) collective-permute-start(bf16[4,7168]{1,0:T(4,128)(2,1)} %refs_2_.1), channel_id=1, source_target_pairs={{0,2},{1,3},{2,0},{3,1},{4,6},{5,7},{6,4},{7,5},{8,10},{9,11},{10,... | collective-permute-start | bytes 172040 | tf_op jit(solution)/shard_map/ppermute | solution.py:202
  17.4 4.4 %collective-permute-start.5 = (bf16[16,7168]{1,0:T(8,128)(2,1)S(1)}, bf16[16,7168]{1,0:T(8,128)(2,1)S(1)}, u32[]{:S(2)}, u32[]{:S(2)}) collective-permute-start(bf16[16,7168]{1,0:T(8,128)(2,1)S(1)} %stack_tokens.3.refs_0_), channel_id=1, source_target_pairs={{0,1},{1,0},{2,3},{3,2},{4,5},{5,4},{6,7},{7,6},{8,9},{9,8},{10,11... | collective-permute-start | bytes 688136 | tf_op jit(solution)/shard_map/ppermute | solution.py:202
  18.0 3.7 %collective-permute-start.6 = (bf16[16,7168]{1,0:T(8,128)(2,1)S(1)}, bf16[16,7168]{1,0:T(8,128)(2,1)S(1)}, u32[]{:S(2)}, u32[]{:S(2)}) collective-permute-start(bf16[16,7168]{1,0:T(8,128)(2,1)S(1)} %stack_tokens.5.refs_1_), channel_id=1, source_target_pairs={{0,1},{1,0},{2,3},{3,2},{4,5},{5,4},{6,7},{7,6},{8,9},{9,8},{10,11... | collective-permute-start | bytes 688136 | tf_op jit(solution)/shard_map/ppermute | solution.py:202
  18.1 11.0 %collective-permute-start.15 = (bf16[336,512]{1,0:T(8,128)(2,1)S(1)}, bf16[336,512]{1,0:T(8,128)(2,1)S(1)}, u32[]{:S(2)}, u32[]{:S(2)}) collective-permute-start(bf16[336,512]{1,0:T(8,128)(2,1)S(1)} %get-tuple-element.25.refs_0_), channel_id=1, source_target_pairs={{0,2},{1,3},{2,0},{3,1},{4,6},{5,7},{6,4},{7,5},{8,10},{9,11},{10,... | collective-permute-start | bytes 1032200 | tf_op jit(solution)/shard_map/ppermute | solution.py:202
  21.8 10.8 %copy-start.2 = (s32[4,2]{0,1:T(2,128)S(1)}, s32[4,2]{0,1:T(2,128)}, u32[]{:S(2)}) copy-start(s32[4,2]{0,1:T(2,128)} %param.9) | copy-start | bytes 100
  24.0 5.6 %collective-permute-start.8 = (bf16[4,16,1792]{2,1,0:T(8,128)(2,1)S(1)}, bf16[4,16,1792]{2,1,0:T(8,128)(2,1)S(1)}, u32[]{:S(2)}, u32[]{:S(2)}) collective-permute-start(bf16[4,16,1792]{2,1,0:T(8,128)(2,1)S(1)} %get-tuple-element.24), channel_id=1, source_target_pairs={{0,1},{1,0},{2,3},{3,2},{4,5},{5,4},{6,7},{7,6},{8,9},{9,8},{10,11... | collective-permute-start | bytes 688136 | tf_op jit(solution)/shard_map/ppermute | solution.py:202
  24.2 16.2 %collective-permute-start.14 = (bf16[448,512]{1,0:T(8,128)(2,1)S(1)}, bf16[448,512]{1,0:T(8,128)(2,1)S(1)}, u32[]{:S(2)}, u32[]{:S(2)}) collective-permute-start(bf16[448,512]{1,0:T(8,128)(2,1)S(1)} %copy-done), channel_id=1, source_target_pairs={{0,1},{1,0},{2,3},{3,2},{4,5},{5,4},{6,7},{7,6},{8,9},{9,8},{10,11... | collective-permute-start | bytes 1376264 | tf_op jit(solution)/shard_map/ppermute | solution.py:202
  24.6 6.7 %collective-permute-start.16 = (bf16[112,512]{1,0:T(8,128)(2,1)S(1)}, bf16[112,512]{1,0:T(8,128)(2,1)S(1)}, u32[]{:S(2)}, u32[]{:S(2)}) collective-permute-start(bf16[112,512]{1,0:T(8,128)(2,1)S(1)} %get-tuple-element.26.refs_1_), channel_id=1, source_target_pairs={{0,2},{1,3},{2,0},{3,1},{4,6},{5,7},{6,4},{7,5},{8,10},{9,11},{10,... | collective-permute-start | bytes 344072 | tf_op jit(solution)/shard_map/ppermute | solution.py:202
  29.1 11.4 %collective-permute-start.17 = (bf16[336,512]{1,0:T(8,128)(2,1)S(1)}, bf16[336,512]{1,0:T(8,128)(2,1)S(1)}, u32[]{:S(2)}, u32[]{:S(2)}) collective-permute-start(bf16[336,512]{1,0:T(8,128)(2,1)S(1)} %collective-permute-done.15.refs_3_), channel_id=1, source_target_pairs={{0,1},{1,0},{2,3},{3,2},{4,5},{5,4},{6,7},{7,6},{8,9},{9,8},{10,11... | collective-permute-start | bytes 1032200 | tf_op jit(solution)/shard_map/ppermute | solution.py:202
  29.1 3.4 %collective-permute-start.7 = (bf16[4,16,1792]{2,1,0:T(8,128)(2,1)S(1)}, bf16[4,16,1792]{2,1,0:T(8,128)(2,1)S(1)}, u32[]{:S(2)}, u32[]{:S(2)}) collective-permute-start(bf16[4,16,1792]{2,1,0:T(8,128)(2,1)S(1)} %get-tuple-element.22), channel_id=1, source_target_pairs={{0,1},{1,0},{2,3},{3,2},{4,5},{5,4},{6,7},{7,6},{8,9},{9,8},{10,11... | collective-permute-start | bytes 688136 | tf_op jit(solution)/shard_map/ppermute | solution.py:202
  29.7 6.1 %collective-permute-start.11 = (bf16[2,16,1792]{2,1,0:T(8,128)(2,1)S(1)}, bf16[2,16,1792]{2,1,0:T(8,128)(2,1)S(1)}, u32[]{:S(2)}, u32[]{:S(2)}) collective-permute-start(bf16[2,16,1792]{2,1,0:T(8,128)(2,1)S(1)} %get-tuple-element.31), channel_id=1, source_target_pairs={{0,2},{1,3},{2,0},{3,1},{4,6},{5,7},{6,4},{7,5},{8,10},{9,11},{10,... | collective-permute-start | bytes 344072 | tf_op jit(solution)/shard_map/ppermute | solution.py:202
  31.3 6.0 %collective-permute-start.9 = (bf16[2,16,1792]{2,1,0:T(8,128)(2,1)S(1)}, bf16[2,16,1792]{2,1,0:T(8,128)(2,1)S(1)}, u32[]{:S(2)}, u32[]{:S(2)}) collective-permute-start(bf16[2,16,1792]{2,1,0:T(8,128)(2,1)S(1)} %get-tuple-element.32), channel_id=1, source_target_pairs={{0,2},{1,3},{2,0},{3,1},{4,6},{5,7},{6,4},{7,5},{8,10},{9,11},{10,... | collective-permute-start | bytes 344072 | tf_op jit(solution)/shard_map/ppermute | solution.py:202
  32.5 5.9 %collective-permute-start.18 = (bf16[112,512]{1,0:T(8,128)(2,1)S(1)}, bf16[112,512]{1,0:T(8,128)(2,1)S(1)}, u32[]{:S(2)}, u32[]{:S(2)}) collective-permute-start(bf16[112,512]{1,0:T(8,128)(2,1)S(1)} %collective-permute-done.16.refs_4_), channel_id=1, source_target_pairs={{0,1},{1,0},{2,3},{3,2},{4,5},{5,4},{6,7},{7,6},{8,9},{9,8},{10,11... | collective-permute-start | bytes 344072 | tf_op jit(solution)/shard_map/ppermute | solution.py:202
  35.8 11.8 %copy-start.1 = (s32[4,2]{0,1:T(2,128)S(1)}, s32[4,2]{0,1:T(2,128)}, u32[]{:S(2)}) copy-start(s32[4,2]{0,1:T(2,128)} %param.8) | copy-start | bytes 100
  35.8 6.7 %collective-permute-start.13 = (bf16[16,1792]{1,0:T(8,128)(2,1)S(1)}, bf16[16,1792]{1,0:T(8,128)(2,1)S(1)}, u32[]{:S(2)}, u32[]{:S(2)}) collective-permute-start(bf16[16,1792]{1,0:T(8,128)(2,1)S(1)} %shard_map.77), channel_id=1, source_target_pairs={{0,12},{1,13},{2,14},{3,15},{4,8},{5,9},{6,10},{7,11},{8,4},{9,5},... | collective-permute-start | bytes 172040 | tf_op jit(solution)/shard_map/ppermute | solution.py:202
  37.3 6.1 %collective-permute-start.12 = (bf16[16,1792]{1,0:T(8,128)(2,1)S(1)}, bf16[16,1792]{1,0:T(8,128)(2,1)S(1)}, u32[]{:S(2)}, u32[]{:S(2)}) collective-permute-start(bf16[16,1792]{1,0:T(8,128)(2,1)S(1)} %shard_map.76), channel_id=1, source_target_pairs={{0,8},{1,9},{2,10},{3,11},{4,12},{5,13},{6,14},{7,15},{8,0},{9,1},... | collective-permute-start | bytes 172040 | tf_op jit(solution)/shard_map/ppermute | solution.py:202
  38.5 4.9 %collective-permute-start.10 = (bf16[16,1792]{1,0:T(8,128)(2,1)S(1)}, bf16[16,1792]{1,0:T(8,128)(2,1)S(1)}, u32[]{:S(2)}, u32[]{:S(2)}) collective-permute-start(bf16[16,1792]{1,0:T(8,128)(2,1)S(1)} %shard_map.75), channel_id=1, source_target_pairs={{0,4},{1,5},{2,6},{3,7},{4,0},{5,1},{6,2},{7,3},{8,12},{9,13},{10,... | collective-permute-start | bytes 172040 | tf_op jit(solution)/shard_map/ppermute | solution.py:202
  43.8 4.7 %collective-permute-start.19 = (f32[8,512]{1,0:T(8,128)S(1)}, f32[8,512]{1,0:T(8,128)S(1)}, u32[]{:S(2)}, u32[]{:S(2)}) collective-permute-start(f32[8,512]{1,0:T(8,128)S(1)} %get-tuple-element.27), channel_id=1, source_target_pairs={{0,8},{1,9},{2,10},{3,11},{4,12},{5,13},{6,14},{7,15},{8,0},{9,1},... | collective-permute-start | bytes 49160 | tf_op jit(solution)/shard_map/ppermute | solution.py:202
  45.0 5.5 %collective-permute-start.20 = (f32[8,512]{1,0:T(8,128)S(1)}, f32[8,512]{1,0:T(8,128)S(1)}, u32[]{:S(2)}, u32[]{:S(2)}) collective-permute-start(f32[8,512]{1,0:T(8,128)S(1)} %get-tuple-element.28), channel_id=1, source_target_pairs={{0,12},{1,13},{2,14},{3,15},{4,8},{5,9},{6,10},{7,11},{8,4},{9,5},... | collective-permute-start | bytes 49160 | tf_op jit(solution)/shard_map/ppermute | solution.py:202
  47.6 3.7 %collective-permute-start.21 = (f32[8,512]{1,0:T(8,128)S(1)}, f32[8,512]{1,0:T(8,128)S(1)}, u32[]{:S(2)}, u32[]{:S(2)}) collective-permute-start(f32[8,512]{1,0:T(8,128)S(1)} %get-tuple-element.29), channel_id=1, source_target_pairs={{0,4},{1,5},{2,6},{3,7},{4,0},{5,1},{6,2},{7,3},{8,12},{9,13},{10,... | collective-permute-start | bytes 49160 | tf_op jit(solution)/shard_map/ppermute | solution.py:202
  (1 other events, 2.5 us)

commit v3 on v2

--- a/solution.py
+++ b/solution.py
@@ -11,7 +11,7 @@
 SLICES = 8
 CORES = 2
 COLUMNS = 2
-MAX_PLANES = 4
+PLANES = 4
 FETCH_PARTS = 8
 LANES = 128
 MIB = 1 << 20
@@ -71,16 +71,20 @@
 
 
 def fetch_kernel(plan, index_ref, *refs):
-    del index_ref
     sources, targets, sems = refs[: -len(plan) - 1], refs[-len(plan) - 1 : -1], refs[-1]
+    group = group_of(index_ref[0])
     copies = []
-    for (operand, first, count), target in zip(plan, targets):
+    for (operand, count), target in zip(plan, targets):
+        source = sources[operand]
         rows = target.shape[0] // count
+        first = 0 if source.shape[0] == target.shape[0] else group * target.shape[0]
         for k in range(count):
-            source = sources[operand].at[pl.ds(first + k * rows, rows), :]
-            sem = sems.at[len(copies)]
-            copies.append(pltpu.make_async_copy(source, target.at[pl.ds(k * rows, rows), :], sem))
-            copies[-1].start()
+            block = pl.ds(first + k * rows, rows)
+            copy = pltpu.make_async_copy(
+                source.at[block, :], target.at[pl.ds(k * rows, rows), :], sems.at[len(copies)]
+            )
+            copy.start()
+            copies.append(copy)
     for copy in copies:
         copy.wait()
 
@@ -98,8 +102,12 @@
         out_ref[n * rows : (n + 1) * rows, :] = block
 
 
+def group_of(index):
+    return jnp.right_shift(index, (CORES * COLUMNS * PLANES).bit_length() - 1)
+
+
 def plane_of(index):
-    return jnp.right_shift(index, (CORES * COLUMNS).bit_length() - 1)
+    return jnp.bitwise_and(jnp.right_shift(index, (CORES * COLUMNS).bit_length() - 1), PLANES - 1)
 
 
 def place_of(index):
@@ -137,15 +145,19 @@
             piece[n] = out[p * quarter : (p + 1) * quarter]
 
 
-def stack_kernel(shard, index_ref, *refs):
-    out_ref = refs[-1]
+def join_kernel(index_ref, own_ref, other_ref, out_ref):
+    rows = own_ref.shape[0]
+    group = group_of(index_ref[0])
+    out_ref[pl.ds(pl.multiple_of(group * rows, rows), rows), :] = own_ref[...]
+    out_ref[pl.ds(pl.multiple_of((1 - group) * rows, rows), rows), :] = other_ref[...]
+
+
+def stack_kernel(index_ref, *refs):
     place = place_of(index_ref[0])
-    taken = 0
-    for part in refs[:-1]:
-        rows = part.shape[0]
-        at = jnp.bitwise_xor(place, taken // shard) * shard + taken % shard
-        out_ref[pl.ds(pl.multiple_of(at, 16), rows), :] = part[...]
-        taken += rows
+    for b, shard in enumerate(refs[:-1]):
+        rows = shard.shape[0]
+        at = pl.multiple_of(jnp.bitwise_xor(place, b) * rows, rows)
+        refs[-1][pl.ds(at, rows), :] = shard[...]
 
 
 def part_total(at, own_ref, other_ref, crossed_ref):
@@ -195,7 +207,7 @@
     quarter = planes * rows
     span = width // planes
     rank = target_basis.shape[1]
-    index = lax.axis_index("expert").astype(jnp.int32).reshape(1)
+    index = lax.axis_index(("group", "expert")).astype(jnp.int32).reshape(1)
     bf16 = jnp.bfloat16
 
     def swap(x, step):
@@ -224,9 +236,9 @@
         operands = [pltpu.with_memory_space_constraint(x, pltpu.HBM) for x in operands]
         targets = [
             pltpu.VMEM((count, operands[operand].shape[1]), operands[operand].dtype)
-            for operand, _, count, _ in plan
+            for operand, count, _ in plan
         ]
-        copies = [(operand, first, count) for operand, first, _, count in plan]
+        copies = [(operand, count) for operand, _, count in plan]
         out = pl.pallas_call(
             functools.partial(fetch_kernel, copies),
             out_shape=tuple(targets),
@@ -238,18 +250,16 @@
         return [pltpu.with_memory_space_constraint(x, pltpu.VMEM) for x in out]
 
     shard = target_basis.shape[0]
-    late = shard // 64 * 16
-    gate, up, own, *basis_parts = fetch(
+    gate, up, own, basis_half = fetch(
         (gate_weight[0], up_weight[0], tokens, target_basis),
         (
-            (0, 0, width, FETCH_PARTS),
-            (1, 0, width, FETCH_PARTS),
-            (2, 0, rows, 1),
-            (3, 0, shard - late, 1),
-            (3, shard - late, late, 1),
+            (0, width, FETCH_PARTS),
+            (1, width, FETCH_PARTS),
+            (2, rows, 1),
+            (3, shard // 2, 1),
         ),
     )
-    (down,) = fetch((down_weight[0],), ((0, 0, down_weight.shape[1], FETCH_PARTS),))
+    (down,) = fetch((down_weight[0],), ((0, down_weight.shape[1], FETCH_PARTS),))
 
     def stack(kernel, shape, blocks):
         return pl.pallas_call(
@@ -281,10 +291,21 @@
     ]
     stacks += [core_swap(tokens_stack) for tokens_stack in stacks]
 
-    column_parts = [column_swap(x) for x in basis_parts]
-    basis_shards = [
-        *basis_parts, core_swap(target_basis), *column_parts, *[core_swap(x) for x in column_parts]
-    ]
+    column_half = column_swap(basis_half)
+    group_half = lax.ppermute(
+        column_half,
+        ("group", "expert"),
+        [(i, (i + devices) % (2 * devices)) for i in range(2 * devices)],
+    )
+    column_basis = pl.pallas_call(
+        join_kernel,
+        out_shape=jax.ShapeDtypeStruct((shard, rank), bf16),
+        in_specs=[smem, vmem, vmem],
+        out_specs=vmem,
+        compiler_params=pltpu.CompilerParams(vmem_limit_bytes=4 * MIB),
+        name="join_basis",
+    )(index, column_half, group_half)
+    basis_shards = [target_basis, core_swap(target_basis), column_basis, core_swap(column_basis)]
 
     piece = jax.ShapeDtypeStruct((planes, quarter, span), bf16)
     pieces = pl.pallas_call(
@@ -298,7 +319,7 @@
     )(index, *stacks, gate, up, down)
 
     basis = pl.pallas_call(
-        functools.partial(stack_kernel, shard),
+        stack_kernel,
         out_shape=jax.ShapeDtypeStruct((width // planes, rank), bf16),
         in_specs=[smem] + [vmem] * len(basis_shards),
         out_specs=vmem,
@@ -351,13 +372,13 @@
     return (
         devices % SLICES == 0
         and SLICES % (CORES * COLUMNS) == 0
-        and planes & (planes - 1) == 0
-        and 1 < planes <= MAX_PLANES
+        and planes == PLANES
+        and lax.axis_size("group") == 2
         and rows & (rows - 1) == 0
         and planes * rows % 16 == 0
         and width % (planes * LANES) == 0
         and target_basis.shape[0] * devices == width
-        and target_basis.shape[0] % 16 == 0
+        and target_basis.shape[0] % 32 == 0
     )
 
 

time: 52.2 us -> 52 us (level)
    ppermute x22 -> x20, waiting for transfers between devices: 20.4 us -> 18.8 us  [swap(): return lax.ppermute(x, 'expert', [(i, i ^ step) for i in range(devices)])]
    ppermute x0 -> x1, waiting for transfers between devices: none -> 1.6 us  [sharded_basis_shards(): lax.ppermute(column_half, ('group', 'expert'), [(i, (i + devices) % (2 *...]
    ppermute x22 -> x20, starting transfers between devices: 22.1 us -> 20.6 us  [swap(): return lax.ppermute(x, 'expert', [(i, i ^ step) for i in range(devices)])]
    ppermute x0 -> x1, starting transfers between devices: none -> 1.49 us  [sharded_basis_shards(): lax.ppermute(column_half, ('group', 'expert'), [(i, (i + devices) % (2 *...]
  transfers between devices with their start and end apart: 22 -> 21, of which waited for: 11 -> 11; matrix products, arithmetic and copies ran while one was open for 0% -> 0% of each run, Pallas kernels for 15% -> 15%
where the time goes in v3:
time: 52 us; the launch traced here: 51.9 us
  starting transfers between devices  22.1 us (42%)
  waiting for transfers between devices  20.4 us (39%)
  Pallas kernels  8.45 us (16%)
  other arithmetic  0.78 us (2%)
    ppermute x20, starting transfers between devices, swap(): return lax.ppermute(x, 'expert', [(i, i ^ step) for i in range(devices)])  20.6 us
    ppermute x20, waiting for transfers between devices, swap(): return lax.ppermute(x, 'expert', [(i, i ^ step) for i in range(devices)])  18.8 us
    pallas_call x2, Pallas kernels, fetch(): pl.pallas_call(functools.partial(fetch_kernel, copies), out_shape=tuple(t...  5.34 us
    pallas_call x1, Pallas kernels, sharded_basis_shards(): pl.pallas_call(functools.partial(expert_kernel, order), out_shape=(piece,...  2.24 us
    ppermute x1, waiting for transfers between devices, sharded_basis_shards(): lax.ppermute(column_half, ('group', 'expert'), [(i, (i + devices) % (2 *...  1.6 us
    ppermute x1, starting transfers between devices, sharded_basis_shards(): lax.ppermute(column_half, ('group', 'expert'), [(i, (i + devices) % (2 *...  1.49 us
  transfers between devices with their start and end apart: 21, of which 11 were waited for; matrix products, arithmetic and copies ran while one was open for 0% of the time, Pallas kernels for 15%

profile of v3, /device:TPU:0, one launch (start us, length us, event | category | flops | bytes accessed | tf_op | source)
XLA Modules:
  0.0 51.9 jit_solution(12168064888755431353)
XLA Ops:
  0.0 3.1 %collective-permute-start = (bf16[4,7168]{1,0:T(4,128)(2,1)}, bf16[4,7168]{1,0:T(4,128)(2,1)S(1)}, u32[]{:S(2)}, u32[]{:S(2)}) collective-permute-start(bf16[4,7168]{1,0:T(4,128)(2,1)} %refs_2_.1), channel_id=1, source_target_pairs={{0,4},{1,5},{2,6},{3,7},{4,0},{5,1},{6,2},{7,3},{8,12},{9,13},{10,... | collective-permute-start | bytes 172040 | tf_op jit(solution)/shard_map/ppermute | solution.py:214
  3.1 2.6 %collective-permute-start.1 = (bf16[4,7168]{1,0:T(4,128)(2,1)}, bf16[4,7168]{1,0:T(4,128)(2,1)S(1)}, u32[]{:S(2)}, u32[]{:S(2)}) collective-permute-start(bf16[4,7168]{1,0:T(4,128)(2,1)} %refs_2_.1), channel_id=1, source_target_pairs={{0,8},{1,9},{2,10},{3,11},{4,12},{5,13},{6,14},{7,15},{8,0},{9,1},... | collective-permute-start | bytes 172040 | tf_op jit(solution)/shard_map/ppermute | solution.py:214
  5.6 3.8 %collective-permute-done.1.refs_2_.refs_1_ = bf16[4,7168]{1,0:T(4,128)(2,1)S(1)} collective-permute-done((bf16[4,7168]{1,0:T(4,128)(2,1)}, bf16[4,7168]{1,0:T(4,128)(2,1)S(1)}, u32[]{:S(2)}, u32[]{:S(2)}) %collective-permute-start.1) | collective-permute-done | bytes 57376 | tf_op jit(solution)/shard_map/ppermute | solution.py:214
  9.5 2.4 %collective-permute-done.2.refs_3_.refs_2_ = bf16[4,7168]{1,0:T(4,128)(2,1)S(1)} collective-permute-done((bf16[4,7168]{1,0:T(4,128)(2,1)}, bf16[4,7168]{1,0:T(4,128)(2,1)S(1)}, u32[]{:S(2)}, u32[]{:S(2)}) %collective-permute-start.2) | collective-permute-done | bytes 57376 | tf_op jit(solution)/shard_map/ppermute | solution.py:214
  11.8 1.6 %collective-permute-start.4 = (bf16[3,4,7168]{2,1,0:T(4,128)(2,1)S(1)}, bf16[3,4,7168]{2,1,0:T(4,128)(2,1)S(1)}, u32[]{:S(2)}, u32[]{:S(2)}) collective-permute-start(bf16[3,4,7168]{2,1,0:T(4,128)(2,1)S(1)} %stack_tokens.4), channel_id=1, source_target_pairs={{0,2},{1,3},{2,0},{3,1},{4,6},{5,7},{6,4},{7,5},{8,10},{9,11},{10,... | collective-permute-start | bytes 516104 | tf_op jit(solution)/shard_map/ppermute | solution.py:214
  13.9 3.3 %shard_map.73 = (bf16[7168,256]{1,0:T(8,128)(2,1)S(1)}, bf16[7168,256]{1,0:T(8,128)(2,1)S(1)}, bf16[4,7168]{1,0:T(4,128)(2,1)S(1)}, bf16[224,512]{1,0:T(8,128)(2,1)S(1)}) custom-call(s32[1]{0:T(128)} %bitcast.index_ref, bf16[7168,256]{1,0:T(8,128)(2,1)} %bitcast.4, bf16[7168,256]{1,0:T(8,128)(2,1)} %bitcast.5, bf16[4,7168]{1,0:T(4,128)(2,1)} %refs_2_.1, ...), custom_call_target="tpu_custom_call" | custom-call | tf_op jit(solution)/shard_map/pallas_call | solution.py:242
  17.2 1.6 %collective-permute-start.15 = (bf16[224,512]{1,0:T(8,128)(2,1)S(1)}, bf16[224,512]{1,0:T(8,128)(2,1)S(1)}, u32[]{:S(2)}, u32[]{:S(2)}) collective-permute-start(bf16[224,512]{1,0:T(8,128)(2,1)S(1)} %get-tuple-element.24), channel_id=1, source_target_pairs={{0,2},{1,3},{2,0},{3,1},{4,6},{5,7},{6,4},{7,5},{8,10},{9,11},{10,... | collective-permute-start | bytes 688136 | tf_op jit(solution)/shard_map/ppermute | solution.py:214
  19.6 2.1 %shard_map.74.refs_6_ = bf16[256,7168]{1,0:T(8,128)(2,1)S(1)} custom-call(s32[1]{0:T(128)} %bitcast.index_ref, bf16[256,7168]{1,0:T(8,128)(2,1)} %bitcast.6), custom_call_target="tpu_custom_call" | custom-call | tf_op jit(solution)/shard_map/pallas_call | solution.py:242
  21.7 1.7 %collective-permute-done.15.own_ref = bf16[224,512]{1,0:T(8,128)(2,1)S(1)} collective-permute-done((bf16[224,512]{1,0:T(8,128)(2,1)S(1)}, bf16[224,512]{1,0:T(8,128)(2,1)S(1)}, u32[]{:S(2)}, u32[]{:S(2)}) %collective-permute-start.15) | collective-permute-done | bytes 229408 | tf_op jit(solution)/shard_map/ppermute | solution.py:214
  23.3 1.5 %collective-permute-start.16 = (bf16[224,512]{1,0:T(8,128)(2,1)S(1)}, bf16[224,512]{1,0:T(8,128)(2,1)S(1)}, u32[]{:S(2)}, u32[]{:S(2)}) collective-permute-start(bf16[224,512]{1,0:T(8,128)(2,1)S(1)} %collective-permute-done.15.own_ref), channel_id=1, source_target_pairs={{0,16},{1,17},{2,18},{3,19},{4,20},{5,21},{6,22},{7,23},{8,24},{9,... | collective-permute-start | bytes 688136 | tf_op jit(solution)/shard_map/ppermute | solution.py:295
  24.8 2.2 %expert_work.1 = (bf16[4,16,1792]{2,1,0:T(8,128)(2,1)S(1)}, bf16[4,16,1792]{2,1,0:T(8,128)(2,1)S(1)}, bf16[4,16,1792]{2,1,0:T(8,128)(2,1)S(1)}, bf16[4,16,1792]{2,1,0:T(8,128)(2,1)S(1)}) custom-call(s32[1]{0:T(128)} %bitcast.index_ref, bf16[16,7168]{1,0:T(8,128)(2,1)S(1)} %stack_tokens.3.refs_0_, bf16[16,7168]{1,0:T(8,128)(2,1)S(1)} %stack_tokens.5.refs_1_, ...), custom_call_target="tpu_custom_call" | custom-call | tf_op jit(solution)/shard_map/expert_work/pallas_call | solution.py:311
  27.7 1.6 %collective-permute-done.16.other_ref = bf16[224,512]{1,0:T(8,128)(2,1)S(1)} collective-permute-done((bf16[224,512]{1,0:T(8,128)(2,1)S(1)}, bf16[224,512]{1,0:T(8,128)(2,1)S(1)}, u32[]{:S(2)}, u32[]{:S(2)}) %collective-permute-start.16) | collective-permute-done | bytes 229408 | tf_op jit(solution)/shard_map/ppermute | solution.py:295
  29.6 1.6 %collective-permute-start.11 = (bf16[2,16,1792]{2,1,0:T(8,128)(2,1)S(1)}, bf16[2,16,1792]{2,1,0:T(8,128)(2,1)S(1)}, u32[]{:S(2)}, u32[]{:S(2)}) collective-permute-start(bf16[2,16,1792]{2,1,0:T(8,128)(2,1)S(1)} %get-tuple-element.29), channel_id=1, source_target_pairs={{0,2},{1,3},{2,0},{3,1},{4,6},{5,7},{6,4},{7,5},{8,10},{9,11},{10,... | collective-permute-start | bytes 344072 | tf_op jit(solution)/shard_map/ppermute | solution.py:214
  31.7 4.0 %collective-permute-done.11.crossed_ref = bf16[2,16,1792]{2,1,0:T(8,128)(2,1)S(1)} collective-permute-done((bf16[2,16,1792]{2,1,0:T(8,128)(2,1)S(1)}, bf16[2,16,1792]{2,1,0:T(8,128)(2,1)S(1)}, u32[]{:S(2)}, u32[]{:S(2)}) %collective-permute-start.11) | collective-permute-done | bytes 114720 | tf_op jit(solution)/shard_map/ppermute | solution.py:214
  35.7 1.3 %collective-permute-start.13 = (bf16[16,1792]{1,0:T(8,128)(2,1)S(1)}, bf16[16,1792]{1,0:T(8,128)(2,1)S(1)}, u32[]{:S(2)}, u32[]{:S(2)}) collective-permute-start(bf16[16,1792]{1,0:T(8,128)(2,1)S(1)} %shard_map.77), channel_id=1, source_target_pairs={{0,12},{1,13},{2,14},{3,15},{4,8},{5,9},{6,10},{7,11},{8,4},{9,5},... | collective-permute-start | bytes 172040 | tf_op jit(solution)/shard_map/ppermute | solution.py:214
  37.6 2.7 %collective-permute-start.10 = (bf16[16,1792]{1,0:T(8,128)(2,1)S(1)}, bf16[16,1792]{1,0:T(8,128)(2,1)S(1)}, u32[]{:S(2)}, u32[]{:S(2)}) collective-permute-start(bf16[16,1792]{1,0:T(8,128)(2,1)S(1)} %shard_map.75), channel_id=1, source_target_pairs={{0,4},{1,5},{2,6},{3,7},{4,0},{5,1},{6,2},{7,3},{8,12},{9,13},{10,... | collective-permute-start | bytes 172040 | tf_op jit(solution)/shard_map/ppermute | solution.py:214
  40.5 1.6 %collective-permute-done.13.refs_2_ = bf16[16,1792]{1,0:T(8,128)(2,1)S(1)} collective-permute-done((bf16[16,1792]{1,0:T(8,128)(2,1)S(1)}, bf16[16,1792]{1,0:T(8,128)(2,1)S(1)}, u32[]{:S(2)}, u32[]{:S(2)}) %collective-permute-start.13) | collective-permute-done | bytes 57376 | tf_op jit(solution)/shard_map/ppermute | solution.py:214
  42.1 1.1 %collective-permute-done.12.refs_1_ = bf16[16,1792]{1,0:T(8,128)(2,1)S(1)} collective-permute-done((bf16[16,1792]{1,0:T(8,128)(2,1)S(1)}, bf16[16,1792]{1,0:T(8,128)(2,1)S(1)}, u32[]{:S(2)}, u32[]{:S(2)}) %collective-permute-start.12) | collective-permute-done | bytes 57376 | tf_op jit(solution)/shard_map/ppermute | solution.py:214
  43.7 1.2 %collective-permute-start.18 = (f32[8,512]{1,0:T(8,128)S(1)}, f32[8,512]{1,0:T(8,128)S(1)}, u32[]{:S(2)}, u32[]{:S(2)}) collective-permute-start(f32[8,512]{1,0:T(8,128)S(1)} %get-tuple-element.25), channel_id=1, source_target_pairs={{0,8},{1,9},{2,10},{3,11},{4,12},{5,13},{6,14},{7,15},{8,0},{9,1},... | collective-permute-start | bytes 49160 | tf_op jit(solution)/shard_map/ppermute | solution.py:214
  44.9 2.6 %collective-permute-start.19 = (f32[8,512]{1,0:T(8,128)S(1)}, f32[8,512]{1,0:T(8,128)S(1)}, u32[]{:S(2)}, u32[]{:S(2)}) collective-permute-start(f32[8,512]{1,0:T(8,128)S(1)} %get-tuple-element.26), channel_id=1, source_target_pairs={{0,12},{1,13},{2,14},{3,15},{4,8},{5,9},{6,10},{7,11},{8,4},{9,5},... | collective-permute-start | bytes 49160 | tf_op jit(solution)/shard_map/ppermute | solution.py:214
  47.5 0.9 %collective-permute-done.18 = f32[8,512]{1,0:T(8,128)S(1)} collective-permute-done((f32[8,512]{1,0:T(8,128)S(1)}, f32[8,512]{1,0:T(8,128)S(1)}, u32[]{:S(2)}, u32[]{:S(2)}) %collective-permute-start.18) | collective-permute-done | bytes 16416 | tf_op jit(solution)/shard_map/ppermute | solution.py:214
  48.4 2.0 %collective-permute-done.19 = f32[8,512]{1,0:T(8,128)S(1)} collective-permute-done((f32[8,512]{1,0:T(8,128)S(1)}, f32[8,512]{1,0:T(8,128)S(1)}, u32[]{:S(2)}, u32[]{:S(2)}) %collective-permute-start.19) | collective-permute-done | bytes 16416 | tf_op jit(solution)/shard_map/ppermute | solution.py:214
  50.4 0.8 %collective-permute-done.20 = f32[8,512]{1,0:T(8,128)S(1)} collective-permute-done((f32[8,512]{1,0:T(8,128)S(1)}, f32[8,512]{1,0:T(8,128)S(1)}, u32[]{:S(2)}, u32[]{:S(2)}) %collective-permute-start.20) | collective-permute-done | bytes 16416 | tf_op jit(solution)/shard_map/ppermute | solution.py:214
  51.2 0.7 %multiply_reduce_fusion = bf16[4,512]{1,0:T(4,128)(2,1)} fusion(f32[2,4,512]{2,1,0:T(4,128)S(1)} %reshape.11, f32[2,4]{1,0:T(2,128)S(1)} %fusion), kind=kLoop, calls=%fused_computation.1 | loop fusion | flops 6144 | bytes 20512 | tf_op jit(solution)/shard_map/reduce_sum | solution.py:365
  (44 shorter events, 4.0 us)
Async XLA Ops:
  0.0 5.6 %collective-permute-start = (bf16[4,7168]{1,0:T(4,128)(2,1)}, bf16[4,7168]{1,0:T(4,128)(2,1)S(1)}, u32[]{:S(2)}, u32[]{:S(2)}) collective-permute-start(bf16[4,7168]{1,0:T(4,128)(2,1)} %refs_2_.1), channel_id=1, source_target_pairs={{0,4},{1,5},{2,6},{3,7},{4,0},{5,1},{6,2},{7,3},{8,12},{9,13},{10,... | collective-permute-start | bytes 172040 | tf_op jit(solution)/shard_map/ppermute | solution.py:214
  3.1 6.4 %collective-permute-start.1 = (bf16[4,7168]{1,0:T(4,128)(2,1)}, bf16[4,7168]{1,0:T(4,128)(2,1)S(1)}, u32[]{:S(2)}, u32[]{:S(2)}) collective-permute-start(bf16[4,7168]{1,0:T(4,128)(2,1)} %refs_2_.1), channel_id=1, source_target_pairs={{0,8},{1,9},{2,10},{3,11},{4,12},{5,13},{6,14},{7,15},{8,0},{9,1},... | collective-permute-start | bytes 172040 | tf_op jit(solution)/shard_map/ppermute | solution.py:214
  5.6 6.2 %collective-permute-start.2 = (bf16[4,7168]{1,0:T(4,128)(2,1)}, bf16[4,7168]{1,0:T(4,128)(2,1)S(1)}, u32[]{:S(2)}, u32[]{:S(2)}) collective-permute-start(bf16[4,7168]{1,0:T(4,128)(2,1)} %refs_2_.1), channel_id=1, source_target_pairs={{0,12},{1,13},{2,14},{3,15},{4,8},{5,9},{6,10},{7,11},{8,4},{9,5},... | collective-permute-start | bytes 172040 | tf_op jit(solution)/shard_map/ppermute | solution.py:214
  11.8 7.1 %collective-permute-start.4 = (bf16[3,4,7168]{2,1,0:T(4,128)(2,1)S(1)}, bf16[3,4,7168]{2,1,0:T(4,128)(2,1)S(1)}, u32[]{:S(2)}, u32[]{:S(2)}) collective-permute-start(bf16[3,4,7168]{2,1,0:T(4,128)(2,1)S(1)} %stack_tokens.4), channel_id=1, source_target_pairs={{0,2},{1,3},{2,0},{3,1},{4,6},{5,7},{6,4},{7,5},{8,10},{9,11},{10,... | collective-permute-start | bytes 516104 | tf_op jit(solution)/shard_map/ppermute | solution.py:214
  13.4 5.5 %collective-permute-start.3 = (bf16[4,7168]{1,0:T(4,128)(2,1)}, bf16[4,7168]{1,0:T(4,128)(2,1)S(1)}, u32[]{:S(2)}, u32[]{:S(2)}) collective-permute-start(bf16[4,7168]{1,0:T(4,128)(2,1)} %refs_2_.1), channel_id=1, source_target_pairs={{0,2},{1,3},{2,0},{3,1},{4,6},{5,7},{6,4},{7,5},{8,10},{9,11},{10,... | collective-permute-start | bytes 172040 | tf_op jit(solution)/shard_map/ppermute | solution.py:214
  17.2 6.1 %collective-permute-start.15 = (bf16[224,512]{1,0:T(8,128)(2,1)S(1)}, bf16[224,512]{1,0:T(8,128)(2,1)S(1)}, u32[]{:S(2)}, u32[]{:S(2)}) collective-permute-start(bf16[224,512]{1,0:T(8,128)(2,1)S(1)} %get-tuple-element.24), channel_id=1, source_target_pairs={{0,2},{1,3},{2,0},{3,1},{4,6},{5,7},{6,4},{7,5},{8,10},{9,11},{10,... | collective-permute-start | bytes 688136 | tf_op jit(solution)/shard_map/ppermute | solution.py:214
  18.9 5.9 %collective-permute-start.5 = (bf16[16,7168]{1,0:T(8,128)(2,1)S(1)}, bf16[16,7168]{1,0:T(8,128)(2,1)S(1)}, u32[]{:S(2)}, u32[]{:S(2)}) collective-permute-start(bf16[16,7168]{1,0:T(8,128)(2,1)S(1)} %stack_tokens.3.refs_0_), channel_id=1, source_target_pairs={{0,1},{1,0},{2,3},{3,2},{4,5},{5,4},{6,7},{7,6},{8,9},{9,8},{10,11... | collective-permute-start | bytes 688136 | tf_op jit(solution)/shard_map/ppermute | solution.py:214
  19.1 5.8 %collective-permute-start.6 = (bf16[16,7168]{1,0:T(8,128)(2,1)S(1)}, bf16[16,7168]{1,0:T(8,128)(2,1)S(1)}, u32[]{:S(2)}, u32[]{:S(2)}) collective-permute-start(bf16[16,7168]{1,0:T(8,128)(2,1)S(1)} %stack_tokens.5.refs_1_), channel_id=1, source_target_pairs={{0,1},{1,0},{2,3},{3,2},{4,5},{5,4},{6,7},{7,6},{8,9},{9,8},{10,11... | collective-permute-start | bytes 688136 | tf_op jit(solution)/shard_map/ppermute | solution.py:214
  23.3 6.0 %collective-permute-start.16 = (bf16[224,512]{1,0:T(8,128)(2,1)S(1)}, bf16[224,512]{1,0:T(8,128)(2,1)S(1)}, u32[]{:S(2)}, u32[]{:S(2)}) collective-permute-start(bf16[224,512]{1,0:T(8,128)(2,1)S(1)} %collective-permute-done.15.own_ref), channel_id=1, source_target_pairs={{0,16},{1,17},{2,18},{3,19},{4,20},{5,21},{6,22},{7,23},{8,24},{9,... | collective-permute-start | bytes 688136 | tf_op jit(solution)/shard_map/ppermute | solution.py:295
  24.8 2.3 %copy-start = (bf16[448,512]{1,0:T(8,128)(2,1)S(1)}, bf16[448,512]{1,0:T(8,128)(2,1)}, u32[]{:S(2)}) copy-start(bf16[448,512]{1,0:T(8,128)(2,1)} %refs_0_.1) | copy-start | bytes 1376260
  24.8 6.8 %copy-start.2 = (s32[4,2]{0,1:T(2,128)S(1)}, s32[4,2]{0,1:T(2,128)}, u32[]{:S(2)}) copy-start(s32[4,2]{0,1:T(2,128)} %param.9) | copy-start | bytes 100
  27.1 2.4 %collective-permute-start.8 = (bf16[4,16,1792]{2,1,0:T(8,128)(2,1)S(1)}, bf16[4,16,1792]{2,1,0:T(8,128)(2,1)S(1)}, u32[]{:S(2)}, u32[]{:S(2)}) collective-permute-start(bf16[4,16,1792]{2,1,0:T(8,128)(2,1)S(1)} %get-tuple-element.23), channel_id=1, source_target_pairs={{0,1},{1,0},{2,3},{3,2},{4,5},{5,4},{6,7},{7,6},{8,9},{9,8},{10,11... | collective-permute-start | bytes 688136 | tf_op jit(solution)/shard_map/ppermute | solution.py:214
  27.2 13.2 %collective-permute-start.14 = (bf16[448,512]{1,0:T(8,128)(2,1)S(1)}, bf16[448,512]{1,0:T(8,128)(2,1)S(1)}, u32[]{:S(2)}, u32[]{:S(2)}) collective-permute-start(bf16[448,512]{1,0:T(8,128)(2,1)S(1)} %copy-done), channel_id=1, source_target_pairs={{0,1},{1,0},{2,3},{3,2},{4,5},{5,4},{6,7},{7,6},{8,9},{9,8},{10,11... | collective-permute-start | bytes 1376264 | tf_op jit(solution)/shard_map/ppermute | solution.py:214
  27.7 4.0 %collective-permute-start.7 = (bf16[4,16,1792]{2,1,0:T(8,128)(2,1)S(1)}, bf16[4,16,1792]{2,1,0:T(8,128)(2,1)S(1)}, u32[]{:S(2)}, u32[]{:S(2)}) collective-permute-start(bf16[4,16,1792]{2,1,0:T(8,128)(2,1)S(1)} %get-tuple-element.21), channel_id=1, source_target_pairs={{0,1},{1,0},{2,3},{3,2},{4,5},{5,4},{6,7},{7,6},{8,9},{9,8},{10,11... | collective-permute-start | bytes 688136 | tf_op jit(solution)/shard_map/ppermute | solution.py:214
  29.4 11.0 %collective-permute-start.17 = (bf16[448,512]{1,0:T(8,128)(2,1)S(1)}, bf16[448,512]{1,0:T(8,128)(2,1)S(1)}, u32[]{:S(2)}, u32[]{:S(2)}) collective-permute-start(bf16[448,512]{1,0:T(8,128)(2,1)S(1)} %join_basis.1.refs_2_), channel_id=1, source_target_pairs={{0,1},{1,0},{2,3},{3,2},{4,5},{5,4},{6,7},{7,6},{8,9},{9,8},{10,11... | collective-permute-start | bytes 1376264 | tf_op jit(solution)/shard_map/ppermute | solution.py:214
  29.6 6.1 %collective-permute-start.11 = (bf16[2,16,1792]{2,1,0:T(8,128)(2,1)S(1)}, bf16[2,16,1792]{2,1,0:T(8,128)(2,1)S(1)}, u32[]{:S(2)}, u32[]{:S(2)}) collective-permute-start(bf16[2,16,1792]{2,1,0:T(8,128)(2,1)S(1)} %get-tuple-element.29), channel_id=1, source_target_pairs={{0,2},{1,3},{2,0},{3,1},{4,6},{5,7},{6,4},{7,5},{8,10},{9,11},{10,... | collective-permute-start | bytes 344072 | tf_op jit(solution)/shard_map/ppermute | solution.py:214
  31.1 6.5 %collective-permute-start.9 = (bf16[2,16,1792]{2,1,0:T(8,128)(2,1)S(1)}, bf16[2,16,1792]{2,1,0:T(8,128)(2,1)S(1)}, u32[]{:S(2)}, u32[]{:S(2)}) collective-permute-start(bf16[2,16,1792]{2,1,0:T(8,128)(2,1)S(1)} %get-tuple-element.30), channel_id=1, source_target_pairs={{0,2},{1,3},{2,0},{3,1},{4,6},{5,7},{6,4},{7,5},{8,10},{9,11},{10,... | collective-permute-start | bytes 344072 | tf_op jit(solution)/shard_map/ppermute | solution.py:214
  35.7 11.8 %copy-start.1 = (s32[4,2]{0,1:T(2,128)S(1)}, s32[4,2]{0,1:T(2,128)}, u32[]{:S(2)}) copy-start(s32[4,2]{0,1:T(2,128)} %param.8) | copy-start | bytes 100
  35.7 6.4 %collective-permute-start.13 = (bf16[16,1792]{1,0:T(8,128)(2,1)S(1)}, bf16[16,1792]{1,0:T(8,128)(2,1)S(1)}, u32[]{:S(2)}, u32[]{:S(2)}) collective-permute-start(bf16[16,1792]{1,0:T(8,128)(2,1)S(1)} %shard_map.77), channel_id=1, source_target_pairs={{0,12},{1,13},{2,14},{3,15},{4,8},{5,9},{6,10},{7,11},{8,4},{9,5},... | collective-permute-start | bytes 172040 | tf_op jit(solution)/shard_map/ppermute | solution.py:214
  37.0 6.1 %collective-permute-start.12 = (bf16[16,1792]{1,0:T(8,128)(2,1)S(1)}, bf16[16,1792]{1,0:T(8,128)(2,1)S(1)}, u32[]{:S(2)}, u32[]{:S(2)}) collective-permute-start(bf16[16,1792]{1,0:T(8,128)(2,1)S(1)} %shard_map.76), channel_id=1, source_target_pairs={{0,8},{1,9},{2,10},{3,11},{4,12},{5,13},{6,14},{7,15},{8,0},{9,1},... | collective-permute-start | bytes 172040 | tf_op jit(solution)/shard_map/ppermute | solution.py:214
  37.6 5.5 %collective-permute-start.10 = (bf16[16,1792]{1,0:T(8,128)(2,1)S(1)}, bf16[16,1792]{1,0:T(8,128)(2,1)S(1)}, u32[]{:S(2)}, u32[]{:S(2)}) collective-permute-start(bf16[16,1792]{1,0:T(8,128)(2,1)S(1)} %shard_map.75), channel_id=1, source_target_pairs={{0,4},{1,5},{2,6},{3,7},{4,0},{5,1},{6,2},{7,3},{8,12},{9,13},{10,... | collective-permute-start | bytes 172040 | tf_op jit(solution)/shard_map/ppermute | solution.py:214
  43.7 4.7 %collective-permute-start.18 = (f32[8,512]{1,0:T(8,128)S(1)}, f32[8,512]{1,0:T(8,128)S(1)}, u32[]{:S(2)}, u32[]{:S(2)}) collective-permute-start(f32[8,512]{1,0:T(8,128)S(1)} %get-tuple-element.25), channel_id=1, source_target_pairs={{0,8},{1,9},{2,10},{3,11},{4,12},{5,13},{6,14},{7,15},{8,0},{9,1},... | collective-permute-start | bytes 49160 | tf_op jit(solution)/shard_map/ppermute | solution.py:214
  44.9 5.5 %collective-permute-start.19 = (f32[8,512]{1,0:T(8,128)S(1)}, f32[8,512]{1,0:T(8,128)S(1)}, u32[]{:S(2)}, u32[]{:S(2)}) collective-permute-start(f32[8,512]{1,0:T(8,128)S(1)} %get-tuple-element.26), channel_id=1, source_target_pairs={{0,12},{1,13},{2,14},{3,15},{4,8},{5,9},{6,10},{7,11},{8,4},{9,5},... | collective-permute-start | bytes 49160 | tf_op jit(solution)/shard_map/ppermute | solution.py:214
  47.4 3.7 %collective-permute-start.20 = (f32[8,512]{1,0:T(8,128)S(1)}, f32[8,512]{1,0:T(8,128)S(1)}, u32[]{:S(2)}, u32[]{:S(2)}) collective-permute-start(f32[8,512]{1,0:T(8,128)S(1)} %get-tuple-element.27), channel_id=1, source_target_pairs={{0,4},{1,5},{2,6},{3,7},{4,0},{5,1},{6,2},{7,3},{8,12},{9,13},{10,... | collective-permute-start | bytes 49160 | tf_op jit(solution)/shard_map/ppermute | solution.py:214
